TPU v7x, 32 devices: a whole 2x2x4 slice. The times are simulated.
32 devices in a mesh: dp: 4 (over z), row: 4 (over y, x), col: 2 (over core).
Axes of the slice: x: 2, y: 2, z: 4, core: 2. Of those that a mesh axis runs over, the one named last changes fastest.
Arguments:
- tokens: bfloat16 [8, 2048, 768], P(('dp', 'col'), 'row'), may hold values from -6 to 6
- cotangent: bfloat16 [8, 2048, 768], P(('dp', 'col'), 'row'), may hold values from -6 to 6
- timesteps: int32 [8], P(('dp', 'col')), may hold values from 0 to 999
- prefix_len: int32 [8], P(('dp', 'col')), may hold values from 204 to 1024, as said below
- time_table: bfloat16 [1000, 768], P('col'), may hold values from -3 to 3
- ln1_gain: float32 [768], replicated, may hold values from 0.25 to 1.75
- ln1_bias: float32 [768], replicated, may hold values from -3 to 3
- w_qkv: bfloat16 [768, 3, 768], P('col', None, 'row'), may hold values from -0.3125 to 0.3125
- w_out: bfloat16 [768, 768], P('col', 'row'), may hold values from -1.75 to 1.75
- out_bias: float32 [768], replicated, may hold values from -3 to 3
- ln2_gain: float32 [768], replicated, may hold values from 0.25 to 1.75
- ln2_bias: float32 [768], replicated, may hold values from -3 to 3
- w_up: bfloat16 [768, 3072], P('col', 'row'), may hold values from -0.21875 to 0.21875
- up_bias: float32 [3072], P('row'), may hold values from -3 to 3
- w_down: bfloat16 [768, 3072], P('col', 'row'), may hold values from -0.109375 to 0.109375
- down_bias: float32 [768], replicated, may hold values from -4 to 4
Outputs:
- layer_out: bfloat16 [8, 2048, 768], P(('dp', 'col'), 'row')
- tokens_grad: float32 [8, 2048, 768], P(('dp', 'col'), 'row')
- table_grad: float32 [1000, 768], P('col')
- ln1_gain_grad: float32 [768], replicated
- ln1_bias_grad: float32 [768], replicated
- qkv_grad: float32 [768, 3, 768], P('col', None, 'row')
- out_grad: float32 [768, 768], P('col', 'row')
- out_bias_grad: float32 [768], replicated
- ln2_gain_grad: float32 [768], replicated
- ln2_bias_grad: float32 [768], replicated
- up_grad: float32 [768, 3072], P('col', 'row')
- up_bias_grad: float32 [3072], P('row')
- down_grad: float32 [768, 3072], P('col', 'row')
- down_bias_grad: float32 [768], replicated
Inputs may be any that keep to these rules, and one draw needn't show every extreme that they name: `prefix_len`: each sequence's prefix length lies between 204 and 1024, and some sequence takes each end.
All inputs are finite; a program needn't handle non-finite values.
Results may differ from a plain program's by a relative error of at most 0.02.
Values may be sent and summed in bfloat16 or wider, within the bound.
A program may use at most 128 MiB of HBM per device.

v0:
```python
import jax
import jax.numpy as jnp
from jax import lax
from jax.sharding import PartitionSpec as P

HD = 64


norm_eps = 1e-05
masked_score = -1e30


def gelu_exact(values):
    return jax.nn.gelu(values, approximate=False)


def gather_rows(values):
    return lax.all_gather(values, "row", axis=1, tiled=True)


def scatter_rows(values):
    return lax.psum_scatter(
        values.astype(jnp.bfloat16), "row", scatter_dimension=1, tiled=True
    ).astype(jnp.float32)


def gather_grads(values):
    return lax.all_gather(values, "row", axis=1, tiled=True)


def scatter_grads(values):
    return lax.psum_scatter(
        values.astype(jnp.bfloat16), "row", scatter_dimension=1, tiled=True
    ).astype(jnp.float32)


def norm_forward(hidden, gain_vec, bias_vec):
    width = hidden.shape[-1]
    average = jnp.sum(hidden, axis=-1, keepdims=True) / width
    variance = jnp.sum(hidden * hidden, axis=-1, keepdims=True) / width - average * average
    inverse = lax.rsqrt(variance + norm_eps)
    centred = (hidden - average) * inverse
    return (centred * gain_vec + bias_vec, centred, inverse)


def norm_backward(grad_out, centred, inverse, gain_vec):
    width = grad_out.shape[-1]
    scaled = grad_out * gain_vec
    first_mean = jnp.sum(scaled, axis=-1, keepdims=True) / width
    second_mean = jnp.sum(scaled * centred, axis=-1, keepdims=True) / width
    grad_in = inverse * (scaled - first_mean - centred * second_mean)
    return (grad_in, jnp.sum(grad_out * centred, axis=(0, 1)), jnp.sum(grad_out, axis=(0, 1)))


def attend_forward(queries, key_rows, values, prefix):
    length = queries.shape[0]
    block_rows = min(512, length)
    score_scale = queries.shape[2] ** (-0.5)
    key_pos = jnp.arange(length, dtype=jnp.int32)

    def one_block(block_index):
        row_start = block_index * block_rows
        query_blk = lax.dynamic_slice_in_dim(queries, row_start, block_rows, 0)
        scores = (
            jnp.einsum("qhd,khd->hqk", query_blk, key_rows, preferred_element_type=jnp.float32)
            * score_scale
        )
        query_pos = row_start + jnp.arange(block_rows, dtype=jnp.int32)
        allowed = (key_pos[None, :] <= query_pos[:, None]) | (key_pos[None, :] < prefix)
        scores = jnp.where(allowed[None], scores, masked_score)
        row_max = jnp.max(scores, axis=2, keepdims=True)
        exponent = jnp.exp(scores - row_max)
        row_total = jnp.sum(exponent, axis=2, keepdims=True)
        soft_low = (exponent / row_total).astype(jnp.bfloat16)
        mixed_blk = jnp.einsum("hqk,khd->qhd", soft_low, values, preferred_element_type=jnp.float32)
        return (mixed_blk, (row_max + jnp.log(row_total))[:, :, 0])

    mixed, logsums = lax.map(one_block, jnp.arange(length // block_rows, dtype=jnp.int32))
    return (mixed.reshape(queries.shape), logsums)


def attend_backward(queries, key_rows, values, mixed, logsums, grad_mixed, prefix):
    length = queries.shape[0]
    block_rows = min(512, length)
    score_scale = queries.shape[2] ** (-0.5)
    key_pos = jnp.arange(length, dtype=jnp.int32)
    delta = jnp.sum(grad_mixed.astype(jnp.float32) * mixed, axis=2)

    def one_block(grads_carry, block_index):
        grad_keys, grad_values = grads_carry
        row_start = block_index * block_rows
        query_blk = lax.dynamic_slice_in_dim(queries, row_start, block_rows, 0)
        grad_blk = lax.dynamic_slice_in_dim(grad_mixed, row_start, block_rows, 0)
        delta_blk = lax.dynamic_slice_in_dim(delta, row_start, block_rows, 0)
        scores = (
            jnp.einsum("qhd,khd->hqk", query_blk, key_rows, preferred_element_type=jnp.float32)
            * score_scale
        )
        query_pos = row_start + jnp.arange(block_rows, dtype=jnp.int32)
        allowed = (key_pos[None, :] <= query_pos[:, None]) | (key_pos[None, :] < prefix)
        scores = jnp.where(allowed[None], scores, masked_score)
        weights_soft = jnp.exp(scores - logsums[block_index][:, :, None])
        grad_soft = jnp.einsum("qhd,khd->hqk", grad_blk, values, preferred_element_type=jnp.float32)
        grad_scores = (weights_soft * (grad_soft - delta_blk.T[:, :, None])).astype(jnp.bfloat16)
        grad_query = (
            jnp.einsum("hqk,khd->qhd", grad_scores, key_rows, preferred_element_type=jnp.float32)
            * score_scale
        )
        grad_keys = (
            grad_keys
            + jnp.einsum("hqk,qhd->khd", grad_scores, query_blk, preferred_element_type=jnp.float32)
            * score_scale
        )
        grad_values = grad_values + jnp.einsum(
            "hqk,qhd->khd",
            weights_soft.astype(jnp.bfloat16),
            grad_blk,
            preferred_element_type=jnp.float32,
        )
        return ((grad_keys, grad_values), grad_query)

    zero_grads = jnp.zeros(key_rows.shape, jnp.float32)
    final_grads, grad_queries = lax.scan(
        one_block, (zero_grads, zero_grads), jnp.arange(length // block_rows, dtype=jnp.int32)
    )
    return jnp.stack([grad_queries.reshape(key_rows.shape), final_grads[0], final_grads[1]], axis=1)


def body(
    tokens,
    cotangent,
    timesteps,
    prefix_len,
    time_table,
    ln1_gain,
    ln1_bias,
    w_qkv,
    w_out,
    out_bias,
    ln2_gain,
    ln2_bias,
    w_up,
    up_bias,
    w_down,
    down_bias,
):
    highest = lax.Precision.HIGHEST
    qkv_full, out_full, up_full, down_full, table_full = (
        lax.all_gather(w_qkv, "col", axis=0, tiled=True),
        lax.all_gather(w_out, "col", axis=0, tiled=True),
        lax.all_gather(w_up, "col", axis=0, tiled=True),
        lax.all_gather(w_down, "col", axis=0, tiled=True),
        lax.all_gather(time_table, "col", axis=0, tiled=True),
    )
    seq_count = tokens.shape[0]
    width_heads = qkv_full.shape[2]
    heads_local = width_heads // HD
    picked = (
        timesteps[:, None] == jnp.arange(table_full.shape[0], dtype=jnp.int32)[None, :]
    ).astype(jnp.float32)
    embed_rows = jnp.dot(picked, table_full.astype(jnp.float32), precision=highest)

    def sequence_forward(seq_item):
        parts_seq, prefix = seq_item
        return attend_forward(parts_seq[:, 0], parts_seq[:, 1], parts_seq[:, 2], prefix)

    def forward_pass(tokens_in):
        hidden0 = tokens_in.astype(jnp.float32) + embed_rows[:, None, :]
        normed1, centred1, inverse1 = norm_forward(hidden0, ln1_gain, ln1_bias)
        full_one = gather_rows(normed1.astype(jnp.bfloat16))
        length = full_one.shape[1]
        project = jnp.einsum(
            "std,dkh->stkh", full_one, qkv_full, preferred_element_type=jnp.float32
        ).astype(jnp.bfloat16)
        parts = project.reshape(seq_count, length, 3, heads_local, HD)
        mixed, logsums = lax.map(sequence_forward, (parts, prefix_len))
        weighted = mixed.reshape(seq_count, length, width_heads).astype(jnp.bfloat16)
        branch = scatter_rows(
            jnp.einsum("sth,dh->std", weighted, out_full, preferred_element_type=jnp.float32)
        )
        hidden1 = hidden0 + (branch + out_bias)
        normed2, centred2, inverse2 = norm_forward(hidden1, ln2_gain, ln2_bias)
        full_two = gather_rows(normed2.astype(jnp.bfloat16))
        inner = (
            jnp.einsum("std,df->stf", full_two, up_full, preferred_element_type=jnp.float32)
            + up_bias
        )
        active = gelu_exact(inner).astype(jnp.bfloat16)
        result = hidden1 + (
            scatter_rows(
                jnp.einsum("stf,df->std", active, down_full, preferred_element_type=jnp.float32)
            )
            + down_bias
        )
        saved = (
            full_one,
            centred1,
            inverse1,
            parts,
            mixed,
            logsums,
            weighted,
            centred2,
            inverse2,
            full_two,
            inner,
            active,
        )
        return (result, saved)

    result, saved = forward_pass(tokens)
    again = lax.optimization_barrier((tokens, result))
    unused, saved = forward_pass(again[0])
    (
        full_one,
        centred1,
        inverse1,
        parts,
        mixed,
        logsums,
        weighted,
        centred2,
        inverse2,
        full_two,
        inner,
        active,
    ) = saved
    length = full_one.shape[1]
    grad_full = gather_grads(cotangent)
    down_grad_full = jnp.einsum(
        "std,stf->df", grad_full, active, preferred_element_type=jnp.float32
    )
    grad_active = jnp.einsum(
        "std,df->stf", grad_full, down_full, preferred_element_type=jnp.float32
    )
    unused_out, gelu_back = jax.vjp(gelu_exact, inner)
    grad_inner = gelu_back(grad_active)[0]
    inner_low = grad_inner.astype(jnp.bfloat16)
    up_grad_full = jnp.einsum(
        "std,stf->df", full_two, inner_low, preferred_element_type=jnp.float32
    )
    grad_normed2 = scatter_grads(
        jnp.einsum("stf,df->std", inner_low, up_full, preferred_element_type=jnp.float32)
    )
    grad_norm_two, ln2_gain_part, ln2_bias_part = norm_backward(
        grad_normed2, centred2, inverse2, ln2_gain
    )
    grad_hidden1 = cotangent.astype(jnp.float32) + grad_norm_two
    grad_branch_full = gather_grads(grad_hidden1.astype(jnp.bfloat16))
    out_grad_full = jnp.einsum(
        "std,sth->dh", grad_branch_full, weighted, preferred_element_type=jnp.float32
    )
    grad_weighted = jnp.einsum(
        "std,dh->sth", grad_branch_full, out_full, preferred_element_type=jnp.float32
    ).astype(jnp.bfloat16)

    def sequence_backward(seq_item):
        parts_seq, mixed_seq, logsum_seq, grad_seq, prefix = seq_item
        return attend_backward(
            parts_seq[:, 0],
            parts_seq[:, 1],
            parts_seq[:, 2],
            mixed_seq,
            logsum_seq,
            grad_seq,
            prefix,
        )

    grad_parts = lax.map(
        sequence_backward,
        (
            parts,
            mixed,
            logsums,
            grad_weighted.reshape(seq_count, length, heads_local, HD),
            prefix_len,
        ),
    )
    grad_project = grad_parts.reshape(seq_count, length, 3, width_heads).astype(jnp.bfloat16)
    qkv_grad_full = jnp.einsum(
        "std,stkh->dkh", full_one, grad_project, preferred_element_type=jnp.float32
    )
    grad_normed1 = scatter_grads(
        jnp.einsum("stkh,dkh->std", grad_project, qkv_full, preferred_element_type=jnp.float32)
    )
    grad_norm_one, ln1_gain_part, ln1_bias_part = norm_backward(
        grad_normed1, centred1, inverse1, ln1_gain
    )
    grad_hidden0 = grad_hidden1 + grad_norm_one
    seq_sums = jnp.sum(grad_hidden0, axis=1)
    table_grad_full = jnp.einsum("sn,sd->nd", picked, seq_sums, precision=highest)
    vectors = lax.psum(
        (
            ln1_gain_part,
            ln1_bias_part,
            jnp.sum(grad_hidden1, axis=(0, 1)),
            ln2_gain_part,
            ln2_bias_part,
            jnp.sum(cotangent.astype(jnp.float32), axis=(0, 1)),
        ),
        ("dp", "row", "col"),
    )
    up_bias_grad = lax.psum(jnp.sum(grad_inner, axis=(0, 1)), ("dp", "col"))
    weights_full = (qkv_grad_full, out_grad_full, up_grad_full, down_grad_full)
    blocks = (
        lax.psum_scatter(
            weights_full[0].astype(jnp.bfloat16), "col", scatter_dimension=0, tiled=True
        ).astype(jnp.float32),
        lax.psum_scatter(
            weights_full[1].astype(jnp.bfloat16), "col", scatter_dimension=0, tiled=True
        ).astype(jnp.float32),
        lax.psum_scatter(
            weights_full[2].astype(jnp.bfloat16), "col", scatter_dimension=0, tiled=True
        ).astype(jnp.float32),
        lax.psum_scatter(
            weights_full[3].astype(jnp.bfloat16), "col", scatter_dimension=0, tiled=True
        ).astype(jnp.float32),
        lax.psum_scatter(
            table_grad_full.astype(jnp.bfloat16), "col", scatter_dimension=0, tiled=True
        ).astype(jnp.float32),
    )
    weight_blocks = (blocks[0], blocks[1], blocks[2], blocks[3])
    weight_blocks = (
        lax.psum(blocks[0].astype(jnp.bfloat16), "dp").astype(jnp.float32),
        lax.psum(blocks[1].astype(jnp.bfloat16), "dp").astype(jnp.float32),
        lax.psum(blocks[2].astype(jnp.bfloat16), "dp").astype(jnp.float32),
        lax.psum(blocks[3].astype(jnp.bfloat16), "dp").astype(jnp.float32),
    )
    table_block = lax.psum(blocks[4].astype(jnp.bfloat16), ("dp", "row")).astype(jnp.float32)
    return (
        result.astype(jnp.bfloat16),
        grad_hidden0,
        table_block,
        vectors[0],
        vectors[1],
        weight_blocks[0],
        weight_blocks[1],
        vectors[2],
        vectors[3],
        vectors[4],
        weight_blocks[2],
        up_bias_grad,
        weight_blocks[3],
        vectors[5],
    )


def solution(mesh):
    placed = (
        P(("dp", "col"), "row", None),
        P(("dp", "col"), "row", None),
        P(("dp", "col")),
        P(("dp", "col")),
        P("col", None),
        P(),
        P(),
        P("col", None, "row"),
        P("col", "row"),
        P(),
        P(),
        P(),
        P("col", "row"),
        P("row"),
        P("col", "row"),
        P(),
    )
    return jax.shard_map(
        body,
        mesh=mesh,
        in_specs=placed,
        out_specs=(
            P(("dp", "col"), "row", None),
            P(("dp", "col"), "row", None),
            P("col", None),
            P(),
            P(),
            P("col", None, "row"),
            P("col", "row"),
            P(),
            P(),
            P(),
            P("col", "row"),
            P("row"),
            P("col", "row"),
            P(),
        ),
        check_vma=False,
    )
```

profile of v0, /device:TPU:15, one launch (start us, length us, event | category | flops | bytes accessed | tf_op | source)
XLA Modules:
  0.0 1126.2 jit_solution(15618841680733205589)
XLA Ops:
  8.7 12.5 %all-gather.27.cloned.1.call-done = bf16[2,500,768]{2,1,0:T(8,128)(2,1)} async-done(((bf16[1,500,768]{2,1,0:T(8,128)(2,1)}), bf16[2,500,768]{2,1,0:T(8,128)(2,1)}) %all-gather.27.cloned.1.call-update) | async-done | bytes 1536016 | tf_op jit(solution)/shard_map/all_gather | solution.py:153
  29.6 39.1 %all-gather.11.cloned.1.call-done = bf16[1,2048,768]{2,1,0:T(8,128)(2,1)} async-done(((bf16[1,512,768]{2,1,0:T(8,128)(2,1)}), bf16[1,2048,768]{2,1,0:T(8,128)(2,1)}) %all-gather.11.cloned.1.call-update) | async-done | bytes 3145744 | tf_op jit(solution)/shard_map/all_gather | solution.py:18
  74.4 78.1 %while.70 = (s32[]{:T(128)}, bf16[4,512,3,64]{1,3,2,0:T(8,128)(2,1)S(1)}, s32[4]{0:T(128)S(1)}, s32[]{:T(128)}, bf16[2048,3,64]{0,2,1:T(8,128)(2,1)}, /*index=5*...) while((s32[]{:T(128)}, ...), condition=%wide.region_5.6_spmd.clone.clone.clone, body=%wide.region_2.5_spmd.clone.clone.sunk.clone | while | flops 826282496 | bytes 29448360 | solution.py:78
  157.3 42.9 %reduce-scatter.18.cloned.1.call-done = bf16[1,512,768]{2,1,0:T(8,128)(2,1)} async-done(((bf16[1,2048,768]{2,1,0:T(8,128)(2,1)}), bf16[1,512,768]{2,1,0:T(8,128)(2,1)}) %reduce-scatter.18.cloned.1.call-update) | async-done | bytes 786448 | tf_op jit(solution)/shard_map/reduce_scatter | solution.py:22
  212.5 11.8 %all-gather.17.cloned.1.call-done = bf16[768,768]{1,0:T(8,128)(2,1)} async-done(((bf16[384,768]{1,0:T(8,128)(2,1)}), bf16[768,768]{1,0:T(8,128)(2,1)}) %all-gather.17.cloned.1.call-update) | async-done | bytes 1179664 | tf_op jit(solution)/shard_map/all_gather | solution.py:152
  224.3 45.8 %all-gather.13.cloned.1.call-done = bf16[1,2048,768]{2,1,0:T(8,128)(2,1)} async-done(((bf16[1,512,768]{2,1,0:T(8,128)(2,1)}), bf16[1,2048,768]{2,1,0:T(8,128)(2,1)}) %all-gather.13.cloned.1.call-update) | async-done | bytes 3145744 | tf_op jit(solution)/shard_map/all_gather | solution.py:18
  270.1 20.8 %fusion.107 = bf16[1,2048,768]{2,1,0:T(8,128)(2,1)} fusion(bf16[768,768]{1,0:T(8,128)(2,1)} %all-gather.17.cloned.1.call-done, bf16[768,768]{1,0:T(8,128)(2,1)} %all-gather.15.cloned.1.call-done, bf16[1,2048,768]{2,1,0:T(8,128)(2,1)} %all-gather.13.cloned.1.call-done, f32[768]{0:T(1024)S(1)} %copy-done.52), kind=kOutput, calls=%fused_computation.139 | convolution fusion | flops 4937220096 | bytes 8653824 | tf_op jit(solution)/shard_map/stf,df->std/dot_general | solution.py:191
  291.0 44.0 %reduce-scatter.20.cloned.1.call-done = bf16[1,512,768]{2,1,0:T(8,128)(2,1)} async-done(((bf16[1,2048,768]{2,1,0:T(8,128)(2,1)}), bf16[1,512,768]{2,1,0:T(8,128)(2,1)}) %reduce-scatter.20.cloned.1.call-update) | async-done | bytes 786448 | tf_op jit(solution)/shard_map/reduce_scatter | solution.py:22
  339.7 43.7 %all-gather.19.cloned.1.call-done = bf16[1,2048,768]{2,1,0:T(8,128)(2,1)} async-done(((bf16[1,512,768]{2,1,0:T(8,128)(2,1)}), bf16[1,2048,768]{2,1,0:T(8,128)(2,1)}) %all-gather.19.cloned.1.call-update) | async-done | bytes 3145744 | tf_op jit(solution)/shard_map/all_gather | solution.py:18
  387.8 91.2 %while.71 = (s32[]{:T(128)}, f32[4,512,3,64]{1,3,2,0:T(8,128)}, f32[4,3,512]{2,1,0:T(4,128)S(1)}, s32[4]{0:T(128)S(1)}, s32[]{:T(128)}, /*index=5*/bf16[2048,3,6...) while((s32[]{:T(128)}, f32[4,512,3,64]{1,3,2,0:T(8,128)}, ...), condition=%wide.region_15.16_spmd.clone.clone.clone, body=%wide.region_12.15_spmd.clone.clone.sunk.clone | while | flops 845153280 | bytes 44169396 | solution.py:78
  485.6 44.0 %reduce-scatter.22.cloned.1.call-done = bf16[1,512,768]{2,1,0:T(8,128)(2,1)} async-done(((bf16[1,2048,768]{2,1,0:T(8,128)(2,1)}), bf16[1,512,768]{2,1,0:T(8,128)(2,1)}) %reduce-scatter.22.cloned.1.call-update) | async-done | bytes 786448 | tf_op jit(solution)/shard_map/reduce_scatter | solution.py:22
  534.8 43.2 %all-gather.21.cloned.1.call-done = bf16[1,2048,768]{2,1,0:T(8,128)(2,1)} async-done(((bf16[1,512,768]{2,1,0:T(8,128)(2,1)}), bf16[1,2048,768]{2,1,0:T(8,128)(2,1)}) %all-gather.21.cloned.1.call-update) | async-done | bytes 3145744 | tf_op jit(solution)/shard_map/all_gather | solution.py:18
  578.0 17.8 %fusion.71 = (f32[2048,768]{1,0:T(8,128)}, f32[2048,768]{1,0:T(8,128)}) fusion(f32[768]{0:T(1024)S(1)} %copy-done.53, bf16[768,768]{1,0:T(8,128)(2,1)S(1)} %copy-done.51, bf16[1,2048,768]{2,1,0:T(8,128)(2,1)} %all-gather.21.cloned.1.call-done), kind=kOutput, calls=%fused_computation.79 | convolution fusion | flops 2515009536 | bytes 16911360 | tf_op jit(solution)/shard_map/std,df->stf/dot_general | solution.py:185
  595.9 28.0 %all-gather.23.cloned.1.call-done = bf16[1,2048,768]{2,1,0:T(8,128)(2,1)} async-done(((bf16[1,512,768]{2,1,0:T(8,128)(2,1)}), bf16[1,2048,768]{2,1,0:T(8,128)(2,1)}) %all-gather.23.cloned.1.call-update) | async-done | bytes 3145744 | tf_op jit(solution)/shard_map/all_gather | solution.py:28
  623.9 11.1 fusion.194
  640.8 44.0 %reduce-scatter.24.cloned.1.call-done = bf16[1,512,768]{2,1,0:T(8,128)(2,1)} async-done(((bf16[1,2048,768]{2,1,0:T(8,128)(2,1)}), bf16[1,512,768]{2,1,0:T(8,128)(2,1)}) %reduce-scatter.24.cloned.1.call-update) | async-done | bytes 786448 | tf_op jit(solution)/shard_map/reduce_scatter | solution.py:32
  704.8 31.9 %all-gather.25.cloned.1.call-done = bf16[1,2048,768]{2,1,0:T(8,128)(2,1)} async-done(((bf16[1,512,768]{2,1,0:T(8,128)(2,1)}), bf16[1,2048,768]{2,1,0:T(8,128)(2,1)}) %all-gather.25.cloned.1.call-update) | async-done | bytes 3145744 | tf_op jit(solution)/shard_map/all_gather | solution.py:28
  746.3 87.0 %while.72 = (s32[]{:T(128)}, f32[2048,3,64]{0,2,1:T(8,128)S(1)}, f32[2048,3,64]{0,2,1:T(8,128)}, bf16[4,512,3,64]{1,3,2,0:T(8,128)(2,1)}, s32[4]{0:T(128)S(1)}, ...) while((s32[]{:T(128)}, f32[2048,3,64]{0,2,1:T(8,128)S(1)}, ...), condition=%wide.region_24.25_spmd.clone.clone.clone, body=%wide.region_23.24_spmd.clone.clone.sunk.clone | while | flops 2048887296 | bytes 79087952 | solution.py:123
  864.3 10.6 reduce-scatter.28.cloned.1.call-done
  875.0 46.3 %reduce-scatter.26.cloned.1.call-done = bf16[1,512,768]{2,1,0:T(8,128)(2,1)} async-done(((bf16[1,2048,768]{2,1,0:T(8,128)(2,1)}), bf16[1,512,768]{2,1,0:T(8,128)(2,1)}) %reduce-scatter.26.cloned.1.call-update) | async-done | bytes 786448 | tf_op jit(solution)/shard_map/reduce_scatter | solution.py:32
  937.1 12.7 %psum.93 = f32[768]{0:T(1024)} all-reduce(f32[768]{0:T(1024)S(1)} %copy-done.48), channel_id=1, replica_groups=mesh['dp'=4,'row'=4,'col'=2] {'dp','col'}, use_global_device_ids=true, to_apply=%region_48.49 | all-reduce | flops 768 | bytes 6144 | tf_op jit(solution)/shard_map/psum | solution.py:303
  949.9 51.9 %all-reduce.9.cloned.1.call-done = (bf16[384,768]{0,1:T(8,128)(2,1)}, bf16[384,3,192]{0,2,1:T(8,128)(2,1)}, bf16[384,192]{0,1:T(8,128)(2,1)}, bf16[384,768]{1,0:T(8,128)(2,1)}) async-done(((bf16[384,768]{0,1:T(8,128)(2,1)}, bf16[384,3,192]{0,2,1:T(8,128)(2,1)}, bf16[384,192]{0,1:T(8,128)(2,1)}, bf16[384,768]{1,0:T(8,128)(2,1)}), (bf16[384,768]{0,1:T(8,128)(2,1)}, bf16[384,3,192]{0,2,1:T(8,128)(2,1)}, ...) | async-done | bytes 1769488 | tf_op jit(solution)/shard_map/psum | solution.py:327
  1008.8 40.7 %all-reduce.2 = (f32[768]{0:T(1024)}, f32[768]{0:T(1024)}, f32[768]{0:T(1024)}, f32[768]{0:T(1024)}, f32[768]{0:T(1024)}, /*index=5*/f32[768]{0:T(1024)}) all-reduce(f32[768]{0:T(1024)S(1)} %get-tuple-element.429, f32[768]{0:T(1024)S(1)} %get-tuple-element.442, ...), channel_id=1, replica_groups=mesh['dp'=4,'row'=4,'col'=2] {'dp','row','col'}, use_global_device_ids=true, to_apply=%region_32.33 | all-reduce | flops 4608 | bytes 36864 | tf_op jit(solution)/shard_map/psum | solution.py:292
  1049.6 67.2 %all-reduce.7.cloned.1.call-done = bf16[500,768]{1,0:T(8,128)(2,1)} async-done(((bf16[500,768]{1,0:T(8,128)(2,1)}), bf16[500,768]{1,0:T(8,128)(2,1)}) %all-reduce.7.cloned.1.call-update) | async-done | bytes 768016 | tf_op jit(solution)/shard_map/psum | solution.py:329
  (355 shorter events, 382.8 us)
Async XLA Ops:
  7.2 14.0 %all-gather.27.cloned.1.call-start = ((), (), s32[]{:S(2)}) async-start(), calls=%async_computation.24 | async-start | bytes 2322432 | tf_op jit(solution)/shard_map/all_gather | solution.py:153
  7.9 60.7 %all-gather.11.cloned.1.call-start = ((), (), s32[]{:S(2)}) async-start(), calls=%async_computation.9 | async-start | bytes 3932160 | tf_op jit(solution)/shard_map/all_gather | solution.py:18
  23.3 664.4 %copy-start.20 = (f32[768]{0:T(1024)}, f32[768]{0:T(1024)S(1)}, u32[]{:S(2)}) copy-start(f32[768]{0:T(1024)S(1)} %convolution_reduce_fusion) | copy-start | bytes 9220
  25.0 175.2 %reduce-scatter.18.cloned.1.call-start = ((), (), s32[]{:S(2)}) async-start(), calls=%async_computation.10 | async-start | bytes 3932160 | tf_op jit(solution)/shard_map/reduce_scatter | solution.py:22
  27.2 126.2 %copy-start.26 = (bf16[768,192]{0,1:T(8,128)(2,1)}, bf16[768,192]{0,1:T(8,128)(2,1)S(1)}, u32[]{:S(2)}) copy-start(bf16[768,192]{0,1:T(8,128)(2,1)S(1)} %all_gather.36) | copy-start | bytes 884740
  156.1 114.0 %copy-start.52 = (f32[768]{0:T(1024)S(1)}, f32[768]{0:T(1024)}, u32[]{:S(2)}) copy-start(f32[768]{0:T(1024)} %param.35) | copy-start | bytes 9220
  156.1 56.4 %all-gather.15.cloned.1.call-start = ((), (), s32[]{:S(2)}) async-start(), calls=%async_computation.12 | async-start | bytes 1769472 | tf_op jit(solution)/shard_map/all_gather | solution.py:151
  156.7 67.6 %all-gather.17.cloned.1.call-start = ((), (), s32[]{:S(2)}) async-start(), calls=%async_computation.13 | async-start | bytes 1769472 | tf_op jit(solution)/shard_map/all_gather | solution.py:152
  157.3 112.8 %all-gather.13.cloned.1.call-start = ((), (), s32[]{:S(2)}) async-start(), calls=%async_computation.11 | async-start | bytes 3932160 | tf_op jit(solution)/shard_map/all_gather | solution.py:18
  204.4 130.6 %reduce-scatter.20.cloned.1.call-start = ((), (), s32[]{:S(2)}) async-start(), calls=%async_computation.14 | async-start | bytes 3932160 | tf_op jit(solution)/shard_map/reduce_scatter | solution.py:22
  291.0 92.4 %all-gather.19.cloned.1.call-start = ((), (), s32[]{:S(2)}) async-start(), calls=%async_computation.15 | async-start | bytes 3932160 | tf_op jit(solution)/shard_map/all_gather | solution.py:18
  339.2 190.4 %reduce-scatter.22.cloned.1.call-start = ((), (), s32[]{:S(2)}) async-start(), calls=%async_computation.16 | async-start | bytes 3932160 | tf_op jit(solution)/shard_map/reduce_scatter | solution.py:22
  485.6 92.4 %all-gather.21.cloned.1.call-start = ((), (), s32[]{:S(2)}) async-start(), calls=%async_computation.17 | async-start | bytes 3932160 | tf_op jit(solution)/shard_map/all_gather | solution.py:18
  533.9 90.0 %all-gather.23.cloned.1.call-start = ((), (), s32[]{:S(2)}) async-start(), calls=%async_computation.18 | async-start | bytes 3932160 | tf_op jit(solution)/shard_map/all_gather | solution.py:28
  534.6 150.3 %reduce-scatter.24.cloned.1.call-start = ((), (), s32[]{:S(2)}) async-start(), calls=%async_computation.19 | async-start | bytes 3932160 | tf_op jit(solution)/shard_map/reduce_scatter | solution.py:32
  640.8 96.0 %all-gather.25.cloned.1.call-start = ((), (), s32[]{:S(2)}) async-start(), calls=%async_computation.20 | async-start | bytes 3932160 | tf_op jit(solution)/shard_map/all_gather | solution.py:28
  692.6 164.2 %reduce-scatter.34.cloned.1.call-start = ((), (), s32[]{:S(2)}) async-start(), calls=%async_computation.27 | async-start | bytes 1769472
  704.8 154.4 %reduce-scatter.32.cloned.1.call-start = ((), (), s32[]{:S(2)}) async-start(), calls=%async_computation.26 | async-start | bytes 589824
  840.4 22.0 %reduce-scatter.30.cloned.1.call-start = ((), (), s32[]{:S(2)}) async-start(), calls=%async_computation.25 | async-start | bytes 1474560
  845.8 29.2 %reduce-scatter.28.cloned.1.call-start = ((), (), s32[]{:S(2)}) async-start(), calls=%async_computation.23 | async-start | bytes 1769472 | tf_op jit(solution)/shard_map/reduce_scatter | solution.py:312
  852.6 68.7 %reduce-scatter.26.cloned.1.call-start = ((), (), s32[]{:S(2)}) async-start(), calls=%async_computation.21 | async-start | bytes 3932160 | tf_op jit(solution)/shard_map/reduce_scatter | solution.py:32
  856.8 144.9 %all-reduce.9.cloned.1.call-start = ((), (), s32[]{:S(2)}) async-start(), calls=%async_computation.28 | async-start | bytes 3538944 | tf_op jit(solution)/shard_map/psum | solution.py:327
  875.0 241.8 %all-reduce.7.cloned.1.call-start = ((), (), s32[]{:S(2)}) async-start(), calls=%async_computation.22 | async-start | bytes 1548288 | tf_op jit(solution)/shard_map/psum | solution.py:329
  931.5 3.1 collective-permute-start
  (61 other events, 1826.7 us)
Sparse Core Ops, SparseCore 0:
  9.6 11.5 all-gather.26
  25.1 43.4 all-gather.10
  156.2 43.9 reduce-scatter.17
  201.6 10.8 all-gather.14
  213.9 10.3 all-gather.16
  226.6 43.4 all-gather.12
  291.1 43.9 reduce-scatter.19
  339.4 43.9 all-gather.18
  485.7 43.9 reduce-scatter.21
  534.0 43.9 all-gather.20
  579.9 43.9 all-gather.22
  640.9 43.9 reduce-scatter.23
  692.7 43.9 all-gather.24
  739.4 10.2 reduce-scatter.33
  840.5 9.4 reduce-scatter.31
  852.6 9.6 reduce-scatter.29
  865.1 9.8 reduce-scatter.27
  877.8 43.5 reduce-scatter.25
  925.1 76.5 all-reduce.8
  1008.3 108.4 all-reduce.6
where the time goes:
time: 1140 us; the launch traced here: 1130 us
  waiting for transfers between devices  620 us (54%)
  matrix products  285 us (25%)
  other arithmetic  84.3 us (7%)
  blocking collectives  62.8 us (6%)
  local copies, waits for them, and re-layouts  38.2 us (3%)
  loops' own time  16.6 us (1%)
  between operations  16.6 us (1%)
    all_gather x4, waiting for transfers between devices, gather_rows(): return lax.all_gather(values, 'row', axis=1, tiled=True)  172 us
    reduce_scatter x3, waiting for transfers between devices, scatter_rows(): lax.psum_scatter(values.astype(jnp.bfloat16), 'row', scatter_dimension=1,...  131 us
    reduce_scatter x2, waiting for transfers between devices, scatter_grads(): lax.psum_scatter(values.astype(jnp.bfloat16), 'row', scatter_dimension=1,...  90.4 us
    psum x1, waiting for transfers between devices, body(): lax.psum(blocks[4].astype(jnp.bfloat16), ('dp', 'row')).astype(jnp.float32)  67.2 us
    all_gather x2, waiting for transfers between devices, gather_grads(): return lax.all_gather(values, 'row', axis=1, tiled=True)  59.9 us
    dot_general x8, matrix products, one_block(): jnp.einsum('hqk,khd->qhd', soft_low, values, preferred_element_type=jnp.f...  56.6 us
    psum x1, waiting for transfers between devices, body(): lax.psum(blocks[3].astype(jnp.bfloat16), 'dp').astype(jnp.float32)  51.9 us
    psum x1, blocking collectives, body(): lax.psum((ln1_gain_part, ln1_bias_part, jnp.sum(grad_hidden1, axis=(0, 1)...  40.7 us
  transfers between devices with their start and end apart: 21, of which 19 were waited for; matrix products, arithmetic and copies ran while one was open for 15% of the time, Pallas kernels for 0%

commit v1 on v0

--- a/solution.py
+++ b/solution.py
@@ -209,8 +209,6 @@
         return (result, saved)
 
     result, saved = forward_pass(tokens)
-    again = lax.optimization_barrier((tokens, result))
-    unused, saved = forward_pass(again[0])
     (
         full_one,
         centred1,

time: 1140 us -> 892 us (0.78)
  waiting for transfers between devices: 620 us -> 482 us
  matrix products: 285 us -> 196 us
  other arithmetic: 84.3 us -> 72.4 us
    all_gather x4 -> x2, waiting for transfers between devices: 172 us -> 84.9 us  [gather_rows(): return lax.all_gather(values, 'row', axis=1, tiled=True)]
    reduce_scatter x3 -> x2, waiting for transfers between devices: 131 us -> 87.3 us  [scatter_rows(): lax.psum_scatter(values.astype(jnp.bfloat16), 'row', scatter_dimension=1,...]
    sub x4 -> x0, matrix products: 40.2 us -> none  [one_block(): exponent = jnp.exp(scores - row_max)]
    dot_general x8 -> x4, matrix products: 56.6 us -> 29.4 us  [one_block(): jnp.einsum('hqk,khd->qhd', soft_low, values, preferred_element_type=jnp.f...]
    dot_general x1, matrix products: 20.8 us -> 6.59 us  [forward_pass(): jnp.einsum('stf,df->std', active, down_full, preferred_element_type=jnp.f...]
    all_gather x2, waiting for transfers between devices: 59.9 us -> 72.8 us  [gather_grads(): return lax.all_gather(values, 'row', axis=1, tiled=True)]
    all_gather x1, waiting for transfers between devices: 11.8 us -> 0.01 us  [body(): lax.all_gather(w_down, 'col', axis=0, tiled=True)]
    unnamed x118 -> x93, local copies, waits for them, and re-layouts: 23.8 us -> 23.4 us
  transfers between devices with their start and end apart: 21 -> 18, of which waited for: 19 -> 15; matrix products, arithmetic and copies ran while one was open for 15% -> 20% of each run, Pallas kernels for 0% -> 0%
where the time goes in v1:
time: 892 us; the launch traced here: 879 us
  waiting for transfers between devices  482 us (54%)
  matrix products  196 us (22%)
  other arithmetic  72.4 us (8%)
  blocking collectives  62.7 us (7%)
  local copies, waits for them, and re-layouts  33.4 us (4%)
  between operations  16.4 us (2%)
  loops' own time  14.1 us (2%)
    reduce_scatter x2, waiting for transfers between devices, scatter_rows(): lax.psum_scatter(values.astype(jnp.bfloat16), 'row', scatter_dimension=1,...  87.3 us
    all_gather x2, waiting for transfers between devices, gather_rows(): return lax.all_gather(values, 'row', axis=1, tiled=True)  84.9 us
    reduce_scatter x2, waiting for transfers between devices, scatter_grads(): lax.psum_scatter(values.astype(jnp.bfloat16), 'row', scatter_dimension=1,...  83.5 us
    all_gather x2, waiting for transfers between devices, gather_grads(): return lax.all_gather(values, 'row', axis=1, tiled=True)  72.8 us
    psum x1, waiting for transfers between devices, body(): lax.psum(blocks[4].astype(jnp.bfloat16), ('dp', 'row')).astype(jnp.float32)  67.2 us
    psum x1, waiting for transfers between devices, body(): lax.psum(blocks[3].astype(jnp.bfloat16), 'dp').astype(jnp.float32)  51.8 us
    psum x1, blocking collectives, body(): lax.psum((ln1_gain_part, ln1_bias_part, jnp.sum(grad_hidden1, axis=(0, 1)...  40.7 us
    dot_general x8, matrix products, one_block(): jnp.einsum('qhd,khd->hqk', query_blk, key_rows, preferred_element_type=jn...  31.4 us
  transfers between devices with their start and end apart: 18, of which 15 were waited for; matrix products, arithmetic and copies ran while one was open for 20% of the time, Pallas kernels for 0%

profile of v1, /device:TPU:15, one launch (start us, length us, event | category | flops | bytes accessed | tf_op | source)
XLA Modules:
  0.0 879.3 jit_solution(11795420427352458064)
XLA Ops:
  8.7 12.5 %all-gather.21.cloned.1.call-done = bf16[2,500,768]{2,1,0:T(8,128)(2,1)} async-done(((bf16[1,500,768]{2,1,0:T(8,128)(2,1)}), bf16[2,500,768]{2,1,0:T(8,128)(2,1)}) %all-gather.21.cloned.1.call-update) | async-done | bytes 1536016 | tf_op jit(solution)/shard_map/all_gather | solution.py:153
  29.5 39.1 %all-gather.9.cloned.1.call-done = bf16[1,2048,768]{2,1,0:T(8,128)(2,1)} async-done(((bf16[1,512,768]{2,1,0:T(8,128)(2,1)}), bf16[1,2048,768]{2,1,0:T(8,128)(2,1)}) %all-gather.9.cloned.1.call-update) | async-done | bytes 3145744 | tf_op jit(solution)/shard_map/all_gather | solution.py:18
  73.2 91.3 %while.50 = (s32[]{:T(128)}, f32[4,512,3,64]{1,3,2,0:T(8,128)}, f32[4,3,512]{2,1,0:T(4,128)S(1)}, s32[4]{0:T(128)S(1)}, s32[]{:T(128)}, /*index=5*/bf16[2048,3,6...) while((s32[]{:T(128)}, f32[4,512,3,64]{1,3,2,0:T(8,128)}, ...), condition=%wide.region_5.6_spmd.clone.clone.clone, body=%wide.region_2.5_spmd.clone.clone.sunk.clone | while | flops 845153280 | bytes 44169396 | solution.py:78
  88.7 7.3 fusion.184
  104.7 6.8 fusion.183
  111.5 7.4 fusion.184
  134.3 7.4 fusion.184
  157.1 7.3 fusion.184
  171.8 43.0 %reduce-scatter.17.cloned.1.call-done = bf16[1,512,768]{2,1,0:T(8,128)(2,1)} async-done(((bf16[1,2048,768]{2,1,0:T(8,128)(2,1)}), bf16[1,512,768]{2,1,0:T(8,128)(2,1)}) %reduce-scatter.17.cloned.1.call-update) | async-done | bytes 786448 | tf_op jit(solution)/shard_map/reduce_scatter | solution.py:22
  227.1 45.8 %all-gather.11.cloned.1.call-done = bf16[1,2048,768]{2,1,0:T(8,128)(2,1)} async-done(((bf16[1,512,768]{2,1,0:T(8,128)(2,1)}), bf16[1,2048,768]{2,1,0:T(8,128)(2,1)}) %all-gather.11.cloned.1.call-update) | async-done | bytes 3145744 | tf_op jit(solution)/shard_map/all_gather | solution.py:18
  272.9 19.0 %multiply_convert_fusion.1 = (bf16[2048,768]{1,0:T(8,128)(2,1)}, f32[2048,768]{1,0:T(8,128)}, f32[2048,768]{1,0:T(8,128)}) fusion(f32[768]{0:T(1024)S(1)} %copy-done.41, bf16[768,768]{1,0:T(8,128)(2,1)} %all-gather.13.cloned.1.call-done, bf16[1,2048,768]{2,1,0:T(8,128)(2,1)} %all-gather.11.cloned.1.call-done), kind=kOutput, calls=%fused_computation.54 | convolution fusion | flops 2519728128 | bytes 20057088 | tf_op jit(solution)/shard_map/std,df->stf/dot_general | solution.py:185
  291.9 38.7 %all-gather.17.cloned.1.call-done = bf16[1,2048,768]{2,1,0:T(8,128)(2,1)} async-done(((bf16[1,512,768]{2,1,0:T(8,128)(2,1)}), bf16[1,2048,768]{2,1,0:T(8,128)(2,1)}) %all-gather.17.cloned.1.call-update) | async-done | bytes 3145744 | tf_op jit(solution)/shard_map/all_gather | solution.py:28
  330.6 11.2 %fusion.112 = (f32[768]{0:T(1024)}, bf16[2048,768]{1,0:T(8,128)(2,1)S(1)}) fusion(f32[2048,768]{1,0:T(8,128)} %get-tuple-element.398, bf16[768,768]{1,0:T(8,128)(2,1)} %all-gather.15.cloned.1.call-done, bf16[1,2048,768]{2,1,0:T(8,128)(2,1)} %all-gather.17.cloned.1.call-done, f32[2048,768]{1,0:T(8,128)} %get-tuple-element.410, f32[768]{0:T(1024)S(1)} %copy-done.41), kind=kOutput, calls=%fused_computation.153 | convolution fusion | flops 2441084160 | bytes 20060160 | tf_op jit(solution)/shard_map/std,df->stf/dot_general | solution.py:231
  354.4 37.2 %reduce-scatter.21.cloned.1.call-done = bf16[1,512,768]{2,1,0:T(8,128)(2,1)} async-done(((bf16[1,2048,768]{2,1,0:T(8,128)(2,1)}), bf16[1,512,768]{2,1,0:T(8,128)(2,1)}) %reduce-scatter.21.cloned.1.call-update) | async-done | bytes 786448 | tf_op jit(solution)/shard_map/reduce_scatter | solution.py:32
  394.3 44.2 %reduce-scatter.19.cloned.1.call-done = bf16[1,512,768]{2,1,0:T(8,128)(2,1)} async-done(((bf16[1,2048,768]{2,1,0:T(8,128)(2,1)}), bf16[1,512,768]{2,1,0:T(8,128)(2,1)}) %reduce-scatter.19.cloned.1.call-update) | async-done | bytes 786448 | tf_op jit(solution)/shard_map/reduce_scatter | solution.py:22
  455.0 34.1 %all-gather.19.cloned.1.call-done = bf16[1,2048,768]{2,1,0:T(8,128)(2,1)} async-done(((bf16[1,512,768]{2,1,0:T(8,128)(2,1)}), bf16[1,2048,768]{2,1,0:T(8,128)(2,1)}) %all-gather.19.cloned.1.call-update) | async-done | bytes 3145744 | tf_op jit(solution)/shard_map/all_gather | solution.py:28
  498.6 87.7 %while.51 = (s32[]{:T(128)}, f32[2048,3,64]{0,2,1:T(8,128)S(1)}, f32[2048,3,64]{0,2,1:T(8,128)}, bf16[4,512,3,64]{1,3,2,0:T(8,128)(2,1)}, s32[4]{0:T(128)S(1)}, ...) while((s32[]{:T(128)}, f32[2048,3,64]{0,2,1:T(8,128)S(1)}, ...), condition=%wide.region_15.16_spmd.clone.clone.clone, body=%wide.region_14.15_spmd.clone.clone.sunk.clone | while | flops 2048887296 | bytes 79087952 | solution.py:123
  599.0 6.8 fusion.92
  617.6 10.7 %reduce-scatter.25.cloned.1.call-done = bf16[384,768]{1,0:T(8,128)(2,1)} async-done(((bf16[768,768]{1,0:T(8,128)(2,1)}), bf16[384,768]{1,0:T(8,128)(2,1)}) %reduce-scatter.25.cloned.1.call-update) | async-done | bytes 589840 | tf_op jit(solution)/shard_map/reduce_scatter | solution.py:310
  628.3 46.3 %reduce-scatter.23.cloned.1.call-done = bf16[1,512,768]{2,1,0:T(8,128)(2,1)} async-done(((bf16[1,2048,768]{2,1,0:T(8,128)(2,1)}), bf16[1,512,768]{2,1,0:T(8,128)(2,1)}) %reduce-scatter.23.cloned.1.call-update) | async-done | bytes 786448 | tf_op jit(solution)/shard_map/reduce_scatter | solution.py:32
  690.4 12.6 %psum.93 = f32[768]{0:T(1024)} all-reduce(f32[768]{0:T(1024)S(1)} %copy-done.37), channel_id=1, replica_groups=mesh['dp'=4,'row'=4,'col'=2] {'dp','col'}, use_global_device_ids=true, to_apply=%region_39.40 | all-reduce | flops 768 | bytes 6144 | tf_op jit(solution)/shard_map/psum | solution.py:301
  703.0 51.8 %all-reduce.9.cloned.1.call-done = (bf16[384,768]{0,1:T(8,128)(2,1)}, bf16[384,3,192]{0,2,1:T(8,128)(2,1)}, bf16[384,192]{0,1:T(8,128)(2,1)}, bf16[384,768]{1,0:T(8,128)(2,1)}) async-done(((bf16[384,768]{0,1:T(8,128)(2,1)}, bf16[384,3,192]{0,2,1:T(8,128)(2,1)}, bf16[384,192]{0,1:T(8,128)(2,1)}, bf16[384,768]{1,0:T(8,128)(2,1)}), (bf16[384,768]{0,1:T(8,128)(2,1)}, bf16[384,3,192]{0,2,1:T(8,128)(2,1)}, ...) | async-done | bytes 1769488 | tf_op jit(solution)/shard_map/psum | solution.py:325
  762.0 40.7 %all-reduce.2 = (f32[768]{0:T(1024)}, f32[768]{0:T(1024)}, f32[768]{0:T(1024)}, f32[768]{0:T(1024)}, f32[768]{0:T(1024)}, /*index=5*/f32[768]{0:T(1024)}) all-reduce(f32[768]{0:T(1024)S(1)} %get-tuple-element.333, f32[768]{0:T(1024)S(1)} %get-tuple-element.342, ...), channel_id=1, replica_groups=mesh['dp'=4,'row'=4,'col'=2] {'dp','row','col'}, use_global_device_ids=true, to_apply=%region_23.24 | all-reduce | flops 4608 | bytes 36864 | tf_op jit(solution)/shard_map/psum | solution.py:290
  802.7 67.2 %all-reduce.7.cloned.1.call-done = bf16[500,768]{1,0:T(8,128)(2,1)} async-done(((bf16[500,768]{1,0:T(8,128)(2,1)}), bf16[500,768]{1,0:T(8,128)(2,1)}) %all-reduce.7.cloned.1.call-update) | async-done | bytes 768016 | tf_op jit(solution)/shard_map/psum | solution.py:327
  (283 shorter events, 251.7 us)
Async XLA Ops:
  7.2 14.0 %all-gather.21.cloned.1.call-start = ((), (), s32[]{:S(2)}) async-start(), calls=%async_computation.20 | async-start | bytes 2322432 | tf_op jit(solution)/shard_map/all_gather | solution.py:153
  7.9 60.7 %all-gather.9.cloned.1.call-start = ((), (), s32[]{:S(2)}) async-start(), calls=%async_computation.8 | async-start | bytes 3932160 | tf_op jit(solution)/shard_map/all_gather | solution.py:18
  23.3 415.3 %copy-start.19 = (f32[768]{0:T(1024)}, f32[768]{0:T(1024)S(1)}, u32[]{:S(2)}) copy-start(f32[768]{0:T(1024)S(1)} %convolution_reduce_fusion) | copy-start | bytes 9220
  25.0 189.8 %reduce-scatter.17.cloned.1.call-start = ((), (), s32[]{:S(2)}) async-start(), calls=%async_computation.9 | async-start | bytes 3932160 | tf_op jit(solution)/shard_map/reduce_scatter | solution.py:22
  170.7 56.4 %all-gather.13.cloned.1.call-start = ((), (), s32[]{:S(2)}) async-start(), calls=%async_computation.11 | async-start | bytes 1769472 | tf_op jit(solution)/shard_map/all_gather | solution.py:151
  171.3 101.6 %copy-start.41 = (f32[768]{0:T(1024)S(1)}, f32[768]{0:T(1024)}, u32[]{:S(2)}) copy-start(f32[768]{0:T(1024)} %param.33) | copy-start | bytes 9220
  171.3 101.6 %all-gather.11.cloned.1.call-start = ((), (), s32[]{:S(2)}) async-start(), calls=%async_computation.10 | async-start | bytes 3932160 | tf_op jit(solution)/shard_map/all_gather | solution.py:18
  219.1 72.8 %all-gather.15.cloned.1.call-start = ((), (), s32[]{:S(2)}) async-start(), calls=%async_computation.12 | async-start | bytes 1769472 | tf_op jit(solution)/shard_map/all_gather | solution.py:152
  219.6 110.9 %all-gather.17.cloned.1.call-start = ((), (), s32[]{:S(2)}) async-start(), calls=%async_computation.14 | async-start | bytes 3932160 | tf_op jit(solution)/shard_map/all_gather | solution.py:28
  220.4 171.2 %reduce-scatter.21.cloned.1.call-start = ((), (), s32[]{:S(2)}) async-start(), calls=%async_computation.15 | async-start | bytes 3932160 | tf_op jit(solution)/shard_map/reduce_scatter | solution.py:32
  347.5 91.1 %reduce-scatter.19.cloned.1.call-start = ((), (), s32[]{:S(2)}) async-start(), calls=%async_computation.13 | async-start | bytes 3932160 | tf_op jit(solution)/shard_map/reduce_scatter | solution.py:22
  354.3 84.3 %copy-start.36 = (f32[768]{0:T(1024)S(1)}, f32[768]{0:T(1024)}, u32[]{:S(2)}) copy-start(f32[768]{0:T(1024)} %param.35) | copy-start | bytes 9220
  354.3 134.8 %all-gather.19.cloned.1.call-start = ((), (), s32[]{:S(2)}) async-start(), calls=%async_computation.16 | async-start | bytes 3932160 | tf_op jit(solution)/shard_map/all_gather | solution.py:28
  445.0 165.1 %reduce-scatter.31.cloned.1.call-start = ((), (), s32[]{:S(2)}) async-start(), calls=%async_computation.23 | async-start | bytes 1769472
  455.0 157.4 %reduce-scatter.29.cloned.1.call-start = ((), (), s32[]{:S(2)}) async-start(), calls=%async_computation.22 | async-start | bytes 589824
  593.5 22.1 %reduce-scatter.27.cloned.1.call-start = ((), (), s32[]{:S(2)}) async-start(), calls=%async_computation.21 | async-start | bytes 1474560
  599.0 29.3 %reduce-scatter.25.cloned.1.call-start = ((), (), s32[]{:S(2)}) async-start(), calls=%async_computation.19 | async-start | bytes 1769472 | tf_op jit(solution)/shard_map/reduce_scatter | solution.py:310
  605.8 68.8 %reduce-scatter.23.cloned.1.call-start = ((), (), s32[]{:S(2)}) async-start(), calls=%async_computation.17 | async-start | bytes 3932160 | tf_op jit(solution)/shard_map/reduce_scatter | solution.py:32
  610.0 144.8 %all-reduce.9.cloned.1.call-start = ((), (), s32[]{:S(2)}) async-start(), calls=%async_computation.24 | async-start | bytes 3538944 | tf_op jit(solution)/shard_map/psum | solution.py:325
  628.3 241.7 %all-reduce.7.cloned.1.call-start = ((), (), s32[]{:S(2)}) async-start(), calls=%async_computation.18 | async-start | bytes 1548288 | tf_op jit(solution)/shard_map/psum | solution.py:327
  684.8 3.1 collective-permute-start
  690.4 71.6 %copy-start.31 = (f32[768]{0:T(1024)S(1)}, f32[768]{0:T(1024)}, u32[]{:S(2)}) copy-start(f32[768]{0:T(1024)} %get-tuple-element.341) | copy-start | bytes 9220
  690.4 71.6 %copy-start.32 = (f32[768]{0:T(1024)S(1)}, f32[768]{0:T(1024)}, u32[]{:S(2)}) copy-start(f32[768]{0:T(1024)} %get-tuple-element.393) | copy-start | bytes 9220
  690.4 71.6 %copy-start.33 = (f32[768]{0:T(1024)S(1)}, f32[768]{0:T(1024)}, u32[]{:S(2)}) copy-start(f32[768]{0:T(1024)} %get-tuple-element.405) | copy-start | bytes 9220
  (46 other events, 978.4 us)
Sparse Core Ops, SparseCore 0:
  9.6 11.5 all-gather.20
  25.1 43.4 all-gather.8
  170.8 43.9 reduce-scatter.16
  216.2 10.8 all-gather.12
  229.4 43.4 all-gather.10
  274.3 10.8 all-gather.14
  287.1 43.4 all-gather.16
  347.6 43.9 reduce-scatter.20
  394.5 43.9 reduce-scatter.18
  445.1 43.9 all-gather.18
  491.9 10.2 reduce-scatter.30
  593.7 9.4 reduce-scatter.28
  606.0 9.6 reduce-scatter.26
  618.4 9.8 reduce-scatter.24
  631.1 43.4 reduce-scatter.22
  678.3 76.5 all-reduce.8
  761.4 108.4 all-reduce.6

commit v2 on v1

v2 whole, which is shorter than its diff:
```python
import functools

import jax
import jax.numpy as jnp
from jax import lax
from jax.experimental import pallas as pl
from jax.experimental.pallas import tpu as pltpu
from jax.sharding import PartitionSpec as P

HD = 64
LANES = 128
norm_eps = 1e-05
masked_score = -1e30
f32, bf16 = jnp.float32, jnp.bfloat16
MESH = pl.DeviceIdType.MESH
NN = (((1,), (0,)), ((), ()))
NT = (((1,), (1,)), ((), ()))
TN = (((0,), (0,)), ((), ()))
VM = pl.BlockSpec(memory_space=pltpu.VMEM)
SM = pl.BlockSpec(memory_space=pltpu.SMEM)
AN = pl.BlockSpec(memory_space=pl.ANY)


def mm(a, b, dims):
    return lax.dot_general(a, b, dims, preferred_element_type=f32)


def remote(src, dst, send, recv, **where):
    return pltpu.make_async_remote_copy(
        src_ref=src, dst_ref=dst, send_sem=send, recv_sem=recv, device_id=where, device_id_type=MESH
    )


def shifted(name, step, count):
    return lax.rem(lax.axis_index(name) + (step + count), count)


def greet(sizes):
    barrier = pltpu.get_barrier_semaphore()
    total = 0
    for name, count in sizes.items():
        for step in range(1, count):
            pl.semaphore_signal(
                barrier, inc=1, device_id={name: shifted(name, step, count)}, device_id_type=MESH
            )
            total += 1
    pl.semaphore_wait(barrier, total)


def other_half(z):
    return z + 1 - 2 * lax.rem(z, 2)


def normalize(hidden, width):
    average = jnp.sum(hidden, axis=-1, keepdims=True) / width
    variance = jnp.sum(hidden * hidden, axis=-1, keepdims=True) / width - average * average
    inverse = lax.rsqrt(variance + norm_eps)
    return (hidden - average) * inverse, inverse


def split_parts(value, lane, count):
    out = jnp.zeros(lane.shape, f32)
    for place in range(count):
        high = value.astype(bf16).astype(f32)
        out = jnp.where(lane == place, high, out)
        value = value - high
    return out.astype(bf16)


def forward_kernel(
    R, C, Z,
    stamp, prefix_ref, x, table, gain, bias, w, wud, wo, ub,
    q, k, v, one, wq, emb, att, mine, wud_all, wo_all, ub_all,
    tab, tabf, o,
    tab_s, tab_r, w_s, w_r, n_s, n_r, a_s, a_r, g_s, g_r, gz_s, gz_r, gc_s, gc_r, wo_s, wo_r, woc_s, woc_r, ub_s, ub_r, loc,
):
    r, c, z = lax.axis_index("row"), lax.axis_index("col"), lax.axis_index("dp")
    T, D = x.shape
    DC = w.shape[0]
    H = w.shape[1] // 3
    heads = H // HD
    L = R * T
    NTB = table.shape[0]
    half = T // 2
    cols = pl.ds(pl.multiple_of(c * DC, DC), DC)
    pair = Z % 2 == 0
    parity = lax.rem(z, 2)

    barrier = pltpu.get_barrier_semaphore()
    total = 0
    for name, count in (("row", R), ("col", C)):
        for step in range(1, count):
            pl.semaphore_signal(barrier, inc=1, device_id={name: shifted(name, step, count)}, device_id_type=MESH)
            total += 1
    if pair:
        pl.semaphore_signal(barrier, inc=1, device_id={"dp": other_half(z)}, device_id_type=MESH)
        total += 1
    pl.semaphore_wait(barrier, total)

    def tab_copy(s):
        return remote(table, tab.at[c], tab_s.at[s - 1], tab_r.at[s - 1], col=shifted("col", s, C))

    def w_copy(s):
        return remote(w, wq.at[cols], w_s.at[s - 1], w_r.at[s - 1], col=shifted("col", s, C))

    def n_copy(s, part):
        piece = one.at[r, pl.ds(part * half, half)]
        return remote(piece, piece, n_s.at[part, s - 1], n_r.at[part, s - 1], row=lax.rem(r + s, R))

    for s in range(1, C):
        tab_copy(s).start()
    for s in range(1, C):
        w_copy(s).start()
    wq[cols, :] = w[...]

    when = stamp[0]

    def pick(block):
        place = when - block * NTB
        inside = (place >= 0) & (place < NTB)
        row = tabf[pl.ds(jnp.clip(place, 0, NTB - 1), 1), :]
        return jnp.where(inside, row, jnp.zeros_like(row))

    tabf[...] = table[...].astype(f32)
    chosen = pick(c)
    for s in range(1, C):
        tab_copy(s).wait_recv()
        block = lax.rem(c - s + C, C)
        tabf[...] = tab[block].astype(f32)
        chosen = chosen + pick(block)
    emb[...] = jnp.broadcast_to(chosen, emb.shape)

    rows_ln = 128
    for part in range(2):

        def norm_step(t, carry, part=part):
            rows = pl.ds(pl.multiple_of(part * half + t * rows_ln, rows_ln), rows_ln)
            hidden = x[rows, :].astype(f32) + chosen
            centred, inverse = normalize(hidden, D)
            one[r, rows, :] = (centred * gain[...] + bias[...]).astype(bf16)
            return carry

        lax.fori_loop(0, half // rows_ln, norm_step, 0)
        for s in range(1, R):
            n_copy(s, part).start()

    which = parity if pair else 0

    def g_copy(s):
        to = lax.rem(r + s, R)
        if pair:
            return remote(wud.at[parity], wud_all.at[parity, r, cols], g_s.at[s - 1], g_r.at[s - 1], row=to)
        return remote(wud, wud_all.at[:, r, cols], g_s.at[s - 1], g_r.at[s - 1], row=to)

    def z_copy(s):
        piece = wud_all.at[parity, lax.rem(r - s + R, R), cols]
        return remote(piece, piece, gz_s.at[s - 1], gz_r.at[s - 1], dp=other_half(z))

    def gc_copy(s, kind, t):
        to = shifted("col", t, C)
        block = lax.rem(r - s + R, R)
        if s == 0:
            return remote(wud, wud_all.at[:, r, cols], gc_s.at[0, 0, t - 1], gc_r.at[0, 0, t - 1], col=to)
        if not pair:
            piece = wud_all.at[:, block, cols]
        else:
            piece = wud_all.at[parity if kind == 0 else 1 - parity, block, cols]
        return remote(piece, piece, gc_s.at[s, kind, t - 1], gc_r.at[s, kind, t - 1], col=to)

    def wo_copy(s):
        return remote(wo, wo_all.at[r, cols], wo_s.at[s - 1], wo_r.at[s - 1], row=lax.rem(r + s, R))

    def woc_copy(s, t):
        to = shifted("col", t, C)
        if s == 0:
            return remote(wo, wo_all.at[r, cols], woc_s.at[0, t - 1], woc_r.at[0, t - 1], col=to)
        piece = wo_all.at[lax.rem(r - s + R, R), cols]
        return remote(piece, piece, woc_s.at[s, t - 1], woc_r.at[s, t - 1], col=to)

    def ub_copy(s):
        return remote(ub, ub_all.at[r], ub_s.at[s - 1], ub_r.at[s - 1], row=lax.rem(r + s, R))

    own_ud = pltpu.make_async_copy(wud, wud_all.at[:, r, cols], loc.at[0])
    own_wo = pltpu.make_async_copy(wo, wo_all.at[r, cols], loc.at[1])
    own_ud.start()
    own_wo.start()
    ub_all[r] = ub[...]
    for s in range(1, R):
        ub_copy(s).start()
        g_copy(s).start()
    for s in range(1, R):
        wo_copy(s).start()
    for t in range(1, C):
        gc_copy(0, 0, t).start()
        woc_copy(0, t).start()

    for s in range(1, C):
        w_copy(s).wait_recv()
    lane = lax.broadcasted_iota(jnp.int32, (T, HD), 1)
    k_tail = jnp.where(lane < 3, 1.0, 0.0).astype(bf16)
    v_tail = jnp.where(lane < 2, 1.0, 0.0).astype(bf16)
    q_tail = jnp.zeros((T, HD), bf16)

    def project(s, carry):
        @pl.when(s > 0)
        def _():
            for part in range(2):
                piece = one.at[r, pl.ds(part * half, half)]
                remote(piece, piece, n_s.at[part, s - 1], n_r.at[part, s - 1], row=lax.rem(r + s, R)).wait_recv()

        block = lax.rem(r - s + R, R)
        y = mm(one[block], wq[...], NN).astype(bf16)
        rows = pl.ds(pl.multiple_of(block * T, T), T)
        scale = HD ** (-0.5)
        for h in range(heads):
            q[h, rows, :] = jnp.concatenate([y[:, h * HD : (h + 1) * HD] * scale, q_tail], axis=1)
            k[h, rows, :] = jnp.concatenate([y[:, H + h * HD : H + (h + 1) * HD], k_tail], axis=1)
            v[h, rows, :] = jnp.concatenate([y[:, 2 * H + h * HD : 2 * H + (h + 1) * HD], v_tail], axis=1)
        return carry

    lax.fori_loop(0, R, project, 0)

    def spread(s):
        g_copy(s).wait_recv()
        if pair:
            z_copy(s).start()
        for t in range(1, C):
            gc_copy(s, 0, t).start()
        wo_copy(s).wait_recv()
        for t in range(1, C):
            woc_copy(s, t).start()

    def spread_pair(s):
        if pair:
            z_copy(s).wait_recv()
            for t in range(1, C):
                gc_copy(s, 1, t).start()

    prefix = prefix_ref[0]
    longest = L // 2
    SB = min(256, T)
    nsub = T // SB
    lane_sb = lax.broadcasted_iota(jnp.int32, (SB, HD), 1)

    def a_copy(i, s):
        return remote(mine.at[i], att.at[r], a_s.at[s - 1], a_r.at[s - 1], row=i)

    for i in range(R):
        early = (i + 1) * T <= longest
        nk = longest if early else (i + 1) * T
        nm = nk if early else T

        def attend(t, carry, i=i, nk=nk, nm=nm):
            h = t // nsub
            sub = pl.multiple_of(lax.rem(t, nsub) * SB, SB)
            row = i * T + sub
            rows = pl.ds(pl.multiple_of(row, SB), SB)
            scores = mm(q[h, rows, :], k[h, :nk, :], NT)
            limit = jnp.maximum(row + 1 + lax.broadcasted_iota(jnp.int32, (SB, 1), 0), prefix)
            place = (nk - nm) + lax.broadcasted_iota(jnp.int32, (SB, nm), 1)
            last = jnp.where(place < limit, scores[:, nk - nm :], masked_score)
            top = jnp.max(last, axis=1, keepdims=True)
            if nk > nm:
                top = jnp.maximum(top, jnp.max(scores[:, : nk - nm], axis=1, keepdims=True))
            mixed = mm(jnp.exp(last - top).astype(bf16), v[h, nk - nm : nk, :], NN)
            if nk > nm:
                mixed += mm(jnp.exp(scores[:, : nk - nm] - top).astype(bf16), v[h, : nk - nm, :], NN)
            weight = mixed[:, HD : HD + 1]
            o[h, pl.ds(sub, SB), :] = mixed / weight
            q[h, rows, HD:] = split_parts(-(top + jnp.log(weight)), lane_sb, 3)
            return carry

        lax.fori_loop(0, heads * nsub, attend, 0)
        mine[i] = jnp.concatenate([o[h][:, :HD] for h in range(heads)], axis=1).astype(bf16)

        @pl.when(r != i)
        def _(i=i):
            a_copy(i, lax.rem(i - r + R, R)).start()

        if 1 <= i < R:
            spread(i)
    att[r] = mine[r]
    for s in range(1, R):
        spread_pair(s)

    for s in range(1, R):
        remote(mine.at[lax.rem(r + s, R)], att.at[r], a_s.at[s - 1], a_r.at[s - 1], row=lax.rem(r + s, R)).wait()
    own_ud.wait()
    own_wo.wait()
    for s in range(1, C):
        tab_copy(s).wait_send()
        w_copy(s).wait_send()
    for s in range(1, R):
        for part in range(2):
            n_copy(s, part).wait_send()
        g_copy(s).wait_send()
        wo_copy(s).wait_send()
        ub_copy(s).wait()
        if pair:
            z_copy(s).wait_send()
    for t in range(1, C):
        for s in range(R):
            gc_copy(s, 0, t).wait()
            if pair and s > 0:
                gc_copy(s, 1, t).wait()
            woc_copy(s, t).wait()


def run_forward(R, C, Z, stamp, prefix, x, table, gain, bias, w, wud, wo, ub):
    T, D = x.shape
    H = w.shape[1] // 3
    F = wud.shape[2]
    heads = H // HD
    L = R * T
    sds = jax.ShapeDtypeStruct
    dma = pltpu.SemaphoreType.DMA
    c1 = max(C - 1, 1)
    sem2 = lambda *shape: [dma(shape), dma(shape)]
    return pl.pallas_call(
        functools.partial(forward_kernel, R, C, Z),
        out_shape=(
            sds((heads, L, LANES), bf16), sds((heads, L, LANES), bf16), sds((heads, L, LANES), bf16),
            sds((R, T, D), bf16), sds((D, 3 * H), bf16), sds((8, D), f32),
            sds((R, T, H), bf16), sds((R, T, H), bf16),
            sds((2, R, D, F), bf16), sds((R, D, H), bf16), sds((R, 1, F), f32),
        ),
        in_specs=[SM, SM] + [VM] * 8,
        out_specs=(VM,) * 8 + (AN, AN, VM),
        scratch_shapes=[
            pltpu.VMEM((C,) + table.shape, bf16), pltpu.VMEM(table.shape, f32), pltpu.VMEM((heads, T, LANES), f32),
        ]
        + sem2(c1) + sem2(c1) + sem2(2, R - 1) + sem2(R - 1) + sem2(R - 1) + sem2(R - 1)
        + sem2(R, 2, c1) + sem2(R - 1) + sem2(R, c1) + sem2(R - 1) + [dma((2,))],
        compiler_params=pltpu.CompilerParams(collective_id=0, has_side_effects=True, vmem_limit_bytes=60 * 2**20),
        name="forward_attention",
    )(stamp, prefix, x, table, gain, bias, w, wud, wo, ub)


def middle_kernel(
    R, C,
    x, cot, emb, att, wud_all, wo_all, ub_all, out_bias, gain, bias, down_bias,
    out, ghid, gatt, gs, gos, vecs, ubg,
    wbuf, hid, acc, gn, n2, n2t, cott, gbuf, crecv, obuf, orecv, gsend,
    wsem, c_s, c_r, o_s, o_r, a_s, a_r,
):
    r, c = lax.axis_index("row"), lax.axis_index("col")
    T, D = x.shape
    F = wud_all.shape[3]
    DC = gs.shape[2]
    TF = 384 if F % 384 == 0 else F
    tiles = F // TF
    cols = pl.ds(pl.multiple_of(c * DC, DC), DC)

    def fetch(s):
        return pltpu.make_async_copy(wud_all.at[:, lax.rem(r + s, R)], wbuf.at[lax.rem(s, 2)], wsem.at[lax.rem(s, 2)])

    fetch(0).start()
    fetch(1).start()
    greet({"row": R, "col": C})

    def c_copy(s, t):
        to = shifted("col", t, C)
        rows = pl.ds(pl.multiple_of(to * DC, DC), DC)
        return remote(gbuf.at[s, :, rows], crecv.at[s, t - 1], c_s.at[s, t - 1], c_r.at[s, t - 1], col=to)

    def o_copy(t):
        to = shifted("col", t, C)
        rows = pl.ds(pl.multiple_of(to * DC, DC), DC)
        return remote(obuf.at[:, rows], orecv.at[t - 1], o_s.at[t - 1], o_r.at[t - 1], col=to)

    TR = min(256, T)
    vsum = jnp.zeros((1, D), f32)
    for part in range(T // TR):
        rows = slice(part * TR, (part + 1) * TR)
        branch = mm(att[0, rows, :], wo_all[0], NT)
        for b in range(1, R):
            branch += mm(att[b, rows, :], wo_all[b], NT)
        hidden = x[rows, :].astype(f32) + emb[0:1, :] + branch + out_bias[...]
        hid[rows, :] = hidden
        centred, inverse = normalize(hidden, D)
        n2[rows, :] = (centred * gain[...] + bias[...]).astype(bf16)
        acc[rows, :] = jnp.zeros((TR, D), f32)
        gn[rows, :] = jnp.zeros((TR, D), f32)
        vsum = vsum + jnp.sum(cot[rows, :].astype(f32), axis=0, keepdims=True)
    n2t[...] = n2[...].T
    cott[...] = cot[...].T
    vecs[5:6, :] = vsum

    def block_step(s, carry):
        slot = lax.rem(s, 2)
        b = lax.rem(r + s, R)
        fetch(s).wait()

        def tile_step(t, inner_carry):
            fcols = pl.ds(pl.multiple_of(t * TF, TF), TF)
            wu = wbuf[slot, 0, :, fcols]
            wd = wbuf[slot, 1, :, fcols]
            inner = mm(n2[...], wu, NN) + ub_all[b, :, fcols]
            cdf = 0.5 * (1.0 + lax.erf(inner * 0.7071067811865476))
            slope = cdf + inner * (jnp.exp(-0.5 * inner * inner) * 0.3989422804014327)
            active = (inner * cdf).astype(bf16)
            acc[...] += mm(active, wd, NT)
            ginner = mm(cot[...], wd, NN) * slope
            glow = ginner.astype(bf16)
            gn[...] += mm(glow, wu, NT)
            gbuf[s, 1, :, fcols] = mm(cott[...], active, NN).astype(bf16)
            gbuf[s, 0, :, fcols] = mm(n2t[...], glow, NN).astype(bf16)
            ubg[b, :, fcols] = jnp.sum(ginner, axis=0, keepdims=True)
            return inner_carry

        lax.fori_loop(0, tiles, tile_step, 0)

        @pl.when(s + 2 < R)
        def _():
            fetch(s + 2).start()

        for t in range(1, C):
            c_copy(s, t).start()

        @pl.when(s > 0)
        def _():
            join(s - 1)

        return carry

    def join(s):
        b = lax.rem(r + s, R)
        for kind in range(2):
            total = gbuf[s, kind, cols, :].astype(f32)
            if kind == 0:
                for t in range(1, C):
                    c_copy(s, t).wait_recv()
            for t in range(1, C):
                total = total + crecv[s, t - 1, kind].astype(f32)
            gs[b, kind] = total.astype(bf16)

    lax.fori_loop(0, R, block_step, 0)

    gain_sum = jnp.zeros((1, D), f32)
    bias_sum = jnp.zeros((1, D), f32)
    hid_sum = jnp.zeros((1, D), f32)
    for part in range(T // TR):
        rows = slice(part * TR, (part + 1) * TR)
        hidden = hid[rows, :]
        out[rows, :] = (hidden + acc[rows, :] + down_bias[...]).astype(bf16)
        centred, inverse = normalize(hidden, D)
        g = gn[rows, :]
        scaled = g * gain[...]
        first = jnp.sum(scaled, axis=-1, keepdims=True) / D
        second = jnp.sum(scaled * centred, axis=-1, keepdims=True) / D
        gh = cot[rows, :].astype(f32) + inverse * (scaled - first - centred * second)
        ghid[rows, :] = gh
        n2[rows, :] = gh.astype(bf16)
        gain_sum = gain_sum + jnp.sum(g * centred, axis=0, keepdims=True)
        bias_sum = bias_sum + jnp.sum(g, axis=0, keepdims=True)
        hid_sum = hid_sum + jnp.sum(gh, axis=0, keepdims=True)
    vecs[0:2, :] = jnp.zeros((2, D), f32)
    vecs[2:3, :] = hid_sum
    vecs[3:4, :] = gain_sum
    vecs[4:5, :] = bias_sum
    vecs[6:8, :] = jnp.zeros((2, D), f32)

    def a_copy(s):
        b = lax.rem(r + s, R)
        return remote(gsend.at[b], gatt.at[r], a_s.at[s - 1], a_r.at[s - 1], row=b)

    def back_step(s, carry):
        b = lax.rem(r + s, R)
        gsend[b] = mm(n2[...], wo_all[b], NN).astype(bf16)

        @pl.when(s < R)
        def _():
            a_copy(s).start()

        return carry

    lax.fori_loop(1, R + 1, back_step, 0)
    gatt[r] = gsend[r]
    n2t[...] = n2[...].T

    def out_step(b, carry):
        obuf[b] = mm(n2t[...], att[b], NN).astype(bf16)
        return carry

    lax.fori_loop(0, R, out_step, 0)
    for t in range(1, C):
        o_copy(t).start()
    join(R - 1)
    for t in range(1, C):
        o_copy(t).wait_recv()
    for b in range(R):
        total = obuf[b, cols, :].astype(f32)
        for t in range(1, C):
            total = total + orecv[t - 1, b].astype(f32)
        gos[b] = total.astype(bf16)
    for s in range(1, R):
        a_copy(s).wait()
    for t in range(1, C):
        o_copy(t).wait_send()
        for s in range(R):
            c_copy(s, t).wait_send()


def run_middle(R, C, DC, x, cot, emb, att, wud_all, wo_all, ub_all, out_bias, gain, bias, down_bias):
    T, D = x.shape
    F = wud_all.shape[3]
    H = wo_all.shape[2]
    sds = jax.ShapeDtypeStruct
    dma = pltpu.SemaphoreType.DMA
    c1 = max(C - 1, 1)
    vm = pltpu.VMEM
    sem2 = lambda *shape: [dma(shape), dma(shape)]
    return pl.pallas_call(
        functools.partial(middle_kernel, R, C),
        out_shape=(
            sds((T, D), bf16), sds((T, D), f32), sds((R, T, H), bf16),
            sds((R, 2, DC, F), bf16), sds((R, DC, H), bf16), sds((8, D), f32), sds((R, 1, F), f32),
        ),
        in_specs=[VM] * 4 + [AN] + [VM] * 6,
        out_specs=(VM,) * 7,
        scratch_shapes=[
            vm((2, 2, D, F), bf16), vm((T, D), f32), vm((T, D), f32), vm((T, D), f32), vm((T, D), bf16),
            vm((D, T), bf16), vm((D, T), bf16), vm((R, 2, D, F), bf16), vm((R, c1, 2, DC, F), bf16),
            vm((R, D, H), bf16), vm((c1, R, DC, H), bf16), vm((R, T, H), bf16),
            dma((2,)),
        ]
        + sem2(R, c1) + sem2(c1) + sem2(R - 1),
        compiler_params=pltpu.CompilerParams(collective_id=1, has_side_effects=True, vmem_limit_bytes=62 * 2**20),
        name="feed_forward",
    )(x, cot, emb, att, wud_all, wo_all, ub_all, out_bias, gain, bias, down_bias)


def backward_kernel(
    R, C, Z,
    stamp, prefix_ref, q, k, v, mine, gatt, one, wq, gs, gos, ubg, vecs, x, emb, gain, ghid,
    tgrad, ffn_out, wo_out, qkv_out, small, table_out,
    d, dq, dk, dv, gp, part, prec, qg, qgb, qrecv, grow, orow, urow, blk, oblk, qblk, zr, zro, zrq,
    vbuf, vrow, vcol, vz,
    g_s, g_r, o_s, o_r, u_s, u_r, p_s, p_r, q_s, q_r, z_s, z_r, y_s, y_r, v_s, v_r, w_s, w_r, t_s, t_r,
):
    r, c, z = lax.axis_index("row"), lax.axis_index("col"), lax.axis_index("dp")
    _, T, H = gatt.shape
    D = x.shape[1]
    heads = H // HD
    L = R * T
    DC = gs.shape[2]
    DZ = blk.shape[1] // Z if zr.shape[2] != blk.shape[1] else blk.shape[1]
    split = DZ != blk.shape[1]
    NTB = table_out.shape[0]
    cols = pl.ds(pl.multiple_of(c * DC, DC), DC)
    greet({"row": R, "col": C, "dp": Z})

    def g_copy(s):
        b = lax.rem(r + s, R)
        return remote(gs.at[b], grow.at[s - 1], g_s.at[s - 1], g_r.at[s - 1], row=b)

    def o_copy(s):
        b = lax.rem(r + s, R)
        return remote(gos.at[b], orow.at[s - 1], o_s.at[s - 1], o_r.at[s - 1], row=b)

    def u_copy(s):
        b = lax.rem(r + s, R)
        return remote(ubg.at[b], urow.at[s - 1], u_s.at[s - 1], u_r.at[s - 1], row=b)

    for s in range(1, R):
        u_copy(s).start()
        g_copy(s).start()
    for s in range(1, R):
        o_copy(s).start()

    lane = lax.broadcasted_iota(jnp.int32, (T, HD), 1)

    def spread_step(b, carry):
        rows = pl.ds(pl.multiple_of(b * T, T), T)
        ga = gatt[b]
        both = ga.astype(f32) * mine[b].astype(f32)
        for h in range(heads):
            piece = slice(h * HD, (h + 1) * HD)
            delta = jnp.sum(both[:, piece], axis=1, keepdims=True)
            d[h, rows, :] = jnp.concatenate([ga[:, piece], split_parts(-delta, lane, 2)], axis=1)
        return carry

    lax.fori_loop(0, R, spread_step, 0)

    dq[...] = jnp.zeros_like(dq)
    dk[...] = jnp.zeros_like(dk)
    dv[...] = jnp.zeros_like(dv)
    prefix = prefix_ref[0]

    def pair(h, i, j, masked):
        qs = pl.ds(pl.multiple_of(i * T, T), T)
        ks = pl.ds(pl.multiple_of(j * T, T), T)
        qb, kb, vb, db = q[h, qs, :], k[h, ks, :], v[h, ks, :], d[h, qs, :]
        scores = mm(kb, qb, NT)
        if masked:
            limit = jnp.maximum(i * T + 1 + lax.broadcasted_iota(jnp.int32, (1, T), 1), prefix)
            place = j * T + lax.broadcasted_iota(jnp.int32, (T, T), 0)
            scores = jnp.where(place < limit, scores, masked_score)
        probs = jnp.exp(scores)
        gscores = (probs * mm(vb, db, NT)).astype(bf16)
        dv[h, ks, :] += mm(probs.astype(bf16), db, NN)
        dk[h, ks, :] += mm(gscores, qb, NN)
        dq[h, qs, :] += mm(gscores, kb, TN)

    def p_copy(b, s):
        return remote(part.at[b], prec.at[s - 1], p_s.at[s - 1], p_r.at[s - 1], row=b)

    def finish(b):
        rows = pl.ds(b * T, T)
        scale = HD ** (-0.5)
        stack = jnp.concatenate(
            [dq[h, rows, :][:, :HD] * scale for h in range(heads)]
            + [dk[h, rows, :][:, :HD] for h in range(heads)]
            + [dv[h, rows, :][:, :HD] for h in range(heads)],
            axis=1,
        ).astype(bf16)
        gp[b] = stack
        part[b] = mm(stack, wq[...], NT).astype(bf16)

        @pl.when(r != b)
        def _():
            p_copy(b, lax.rem(b - r + R, R)).start()

    early = R // 2
    for i in range(R - 1, early - 1, -1):

        def plain(t, carry, i=i):
            pair(t // i, i, lax.rem(t, i), False)
            return carry

        def diagonal(h, carry, i=i):
            pair(h, i, i, True)
            return carry

        lax.fori_loop(0, heads * i, plain, 0)
        lax.fori_loop(0, heads, diagonal, 0)
        finish(i)

    def square(t, carry):
        rest = lax.rem(t, early * early)
        pair(t // (early * early), rest // early, lax.rem(rest, early), True)
        return carry

    lax.fori_loop(0, heads * early * early, square, 0)
    for b in range(early - 1, -1, -1):
        finish(b)

    qg[...] = jnp.zeros_like(qg)

    def qkv_step(b, carry):
        qg[...] += mm(one[b], gp[b], TN)
        return carry

    lax.fori_loop(0, R, qkv_step, 0)
    qgb[...] = qg[...].astype(bf16)

    def q_copy(t):
        to = shifted("col", t, C)
        rows = pl.ds(pl.multiple_of(to * DC, DC), DC)
        return remote(qgb.at[rows], qrecv.at[t - 1], q_s.at[t - 1], q_r.at[t - 1], col=to)

    for t in range(1, C):
        q_copy(t).start()

    def z_copy(kind, s):
        to = lax.rem(z + s, Z)
        rows = pl.ds(pl.multiple_of(to * DZ, DZ), DZ) if split else slice(None)
        source, target = ((blk, zr), (oblk, zro), (qblk, zrq))[kind]
        if kind == 0:
            return remote(source.at[:, rows], target.at[s - 1], z_s.at[kind, s - 1], z_r.at[kind, s - 1], dp=to)
        return remote(source.at[rows], target.at[s - 1], z_s.at[kind, s - 1], z_r.at[kind, s - 1], dp=to)

    def y_copy(kind, s):
        to = lax.rem(z + s, Z)
        rows = pl.ds(pl.multiple_of(z * DZ, DZ), DZ)
        ref = (ffn_out, wo_out, qkv_out)[kind]
        piece = ref.at[:, rows] if kind == 0 else ref.at[rows]
        return remote(piece, piece, y_s.at[kind, s - 1], y_r.at[kind, s - 1], dp=to)

    def reduce_data(kind):
        for s in range(1, Z):
            z_copy(kind, s).wait_recv()
        rows = pl.ds(pl.multiple_of(z * DZ, DZ), DZ) if split else slice(None)
        source, target = ((blk, zr), (oblk, zro), (qblk, zrq))[kind]
        ref = (ffn_out, wo_out, qkv_out)[kind]
        for array in range(2 if kind == 0 else 1):
            where = (array, rows) if kind == 0 else (rows,)
            total = source[where].astype(f32)
            for s in range(1, Z):
                got = target[s - 1, array] if kind == 0 else target[s - 1]
                total = total + got.astype(f32)
            ref[where] = total.astype(bf16)
        if split:
            for s in range(1, Z):
                y_copy(kind, s).start()

    for s in range(1, R):
        g_copy(s).wait_recv()
    for array in range(2):
        total = gs[r, array].astype(f32)
        for s in range(1, R):
            total = total + grow[s - 1, array].astype(f32)
        blk[array] = total.astype(bf16)
    for s in range(1, Z):
        z_copy(0, s).start()
    for s in range(1, R):
        o_copy(s).wait_recv()
    total = gos[r].astype(f32)
    for s in range(1, R):
        total = total + orow[s - 1].astype(f32)
    oblk[...] = total.astype(bf16)
    for s in range(1, Z):
        z_copy(1, s).start()
    for t in range(1, C):
        q_copy(t).wait_recv()
    total = qgb[cols, :].astype(f32)
    for t in range(1, C):
        total = total + qrecv[t - 1].astype(f32)
    qblk[...] = total.astype(bf16)
    for s in range(1, Z):
        z_copy(2, s).start()
    reduce_data(0)

    for s in range(1, R):
        remote(part.at[0], prec.at[s - 1], p_s.at[s - 1], p_r.at[s - 1], row=lax.rem(r + s, R)).wait_recv()
        u_copy(s).wait_recv()
    TR = min(256, T)
    gain_sum = jnp.zeros((1, D), f32)
    bias_sum = jnp.zeros((1, D), f32)
    all_sum = jnp.zeros((1, D), f32)
    for piece in range(T // TR):
        rows = slice(piece * TR, (piece + 1) * TR)
        g = part[r, rows, :].astype(f32)
        for s in range(1, R):
            g = g + prec[s - 1, rows, :].astype(f32)
        centred, inverse = normalize(x[rows, :].astype(f32) + emb[0:1, :], D)
        scaled = g * gain[...]
        first = jnp.sum(scaled, axis=-1, keepdims=True) / D
        second = jnp.sum(scaled * centred, axis=-1, keepdims=True) / D
        total = ghid[rows, :] + inverse * (scaled - first - centred * second)
        tgrad[rows, :] = total
        gain_sum = gain_sum + jnp.sum(g * centred, axis=0, keepdims=True)
        bias_sum = bias_sum + jnp.sum(g, axis=0, keepdims=True)
        all_sum = all_sum + jnp.sum(total, axis=0, keepdims=True)

    vbuf[...] = vecs[...]
    vbuf[0:1, :] = gain_sum
    vbuf[1:2, :] = bias_sum
    vbuf[6:7, :] = all_sum

    def v_copy(s):
        return remote(vbuf, vrow.at[s - 1], v_s.at[s - 1], v_r.at[s - 1], row=lax.rem(r + s, R))

    for s in range(1, R):
        v_copy(s).start()
    reduce_data(1)
    reduce_data(2)
    up_bias = ubg[r]
    for s in range(1, R):
        up_bias = up_bias + urow[s - 1]
    for s in range(1, R):
        v_copy(s).wait_recv()
    total = vbuf[...]
    for s in range(1, R):
        total = total + vrow[s - 1]
    vcol[c, 0:8, :] = total
    vcol[c, 7:8, :] = up_bias
    vcol[c, 8:16, :] = jnp.full((8, D), stamp[0].astype(f32))

    def w_copy(t):
        return remote(vcol.at[c], vcol.at[c], w_s.at[t - 1], w_r.at[t - 1], col=shifted("col", t, C))

    for t in range(1, C):
        w_copy(t).start()
    for t in range(1, C):
        w_copy(t).wait_recv()

    def t_copy(s):
        return remote(vcol, vz.at[s - 1], t_s.at[s - 1], t_r.at[s - 1], dp=lax.rem(z + s, Z))

    for s in range(1, Z):
        t_copy(s).start()
    for s in range(1, Z):
        t_copy(s).wait_recv()
    total = jnp.zeros((8, D), f32)
    number = (lax.broadcasted_iota(jnp.int32, (NTB, D), 0) + c * NTB).astype(f32)
    table = jnp.zeros((NTB, D), f32)
    for s in range(Z):
        for t in range(C):
            entry = vcol[t] if s == 0 else vz[s - 1, t]
            total = total + entry[0:8]
            table = table + jnp.where(number == entry[8:9], entry[6:7], 0.0)
    small[...] = total
    table_out[...] = table

    for s in range(1, R):
        g_copy(s).wait_send()
        o_copy(s).wait_send()
        u_copy(s).wait_send()
        v_copy(s).wait_send()
        remote(part.at[0], prec.at[s - 1], p_s.at[s - 1], p_r.at[s - 1], row=lax.rem(r + s, R)).wait_send()
    for t in range(1, C):
        q_copy(t).wait_send()
        w_copy(t).wait_send()
    for s in range(1, Z):
        t_copy(s).wait_send()
        for kind in range(3):
            z_copy(kind, s).wait_send()
            if split:
                y_copy(kind, s).wait()


def run_backward(R, C, Z, NTB, stamp, prefix, q, k, v, mine, gatt, one, wq, gs, gos, ubg, vecs, x, emb, gain, ghid):
    T, D = x.shape
    H = gatt.shape[2]
    heads = H // HD
    L = R * T
    DC, F = gs.shape[2], gs.shape[3]
    DZ = DC // Z if DC % (16 * Z) == 0 else DC
    sds = jax.ShapeDtypeStruct
    dma = pltpu.SemaphoreType.DMA
    c1 = max(C - 1, 1)
    vm = pltpu.VMEM
    sem2 = lambda *shape: [dma(shape), dma(shape)]
    return pl.pallas_call(
        functools.partial(backward_kernel, R, C, Z),
        out_shape=(
            sds((T, D), f32), sds((2, DC, F), bf16), sds((DC, H), bf16), sds((DC, 3 * H), bf16),
            sds((8, D), f32), sds((NTB, D), f32),
        ),
        in_specs=[SM, SM] + [VM] * 15,
        out_specs=(VM,) * 6,
        scratch_shapes=[
            vm((heads, L, LANES), bf16), vm((heads, L, LANES), f32), vm((heads, L, LANES), f32), vm((heads, L, LANES), f32),
            vm((R, T, 3 * H), bf16), vm((R, T, D), bf16), vm((R - 1, T, D), bf16), vm((D, 3 * H), f32), vm((D, 3 * H), bf16),
            vm((c1, DC, 3 * H), bf16), vm((R - 1, 2, DC, F), bf16), vm((R - 1, DC, H), bf16), vm((R - 1, 1, F), f32),
            vm((2, DC, F), bf16), vm((DC, H), bf16), vm((DC, 3 * H), bf16),
            vm((Z - 1, 2, DZ, F), bf16), vm((Z - 1, DZ, H), bf16), vm((Z - 1, DZ, 3 * H), bf16),
            vm((8, D), f32), vm((R - 1, 8, D), f32), vm((C, 16, D), f32), vm((Z - 1, C, 16, D), f32),
        ]
        + sem2(R - 1) * 4 + sem2(c1) + sem2(3, Z - 1) + sem2(3, Z - 1) + sem2(R - 1) + sem2(c1) + sem2(Z - 1),
        compiler_params=pltpu.CompilerParams(collective_id=2, has_side_effects=True, vmem_limit_bytes=63 * 2**20),
        name="backward_attention",
    )(stamp, prefix, q, k, v, mine, gatt, one, wq, gs, gos, ubg, vecs, x, emb, gain, ghid)


def body(R, C, Z, *args):
    (tokens, cotangent, timesteps, prefix_len, time_table, ln1_gain, ln1_bias, w_qkv, w_out, out_bias,
     ln2_gain, ln2_bias, w_up, up_bias, w_down, down_bias) = args
    DC, _, H = w_qkv.shape
    D = tokens.shape[2]
    x, cot = tokens[0], cotangent[0]
    row = lambda vector: vector[None, :]
    q, k, v, one, wq, emb, att, mine, wud_all, wo_all, ub_all = run_forward(
        R, C, Z, timesteps, prefix_len, x, time_table, row(ln1_gain), row(ln1_bias),
        w_qkv.reshape(DC, 3 * H), jnp.stack([w_up, w_down]), w_out, row(up_bias),
    )
    out, ghid, gatt, gs, gos, vecs, ubg = run_middle(
        R, C, DC, x, cot, emb, att, wud_all, wo_all, ub_all,
        row(out_bias), row(ln2_gain), row(ln2_bias), row(down_bias),
    )
    tgrad, ffn, wo, qkv, small, table = run_backward(
        R, C, Z, time_table.shape[0], timesteps, prefix_len, q, k, v, mine, gatt, one, wq, gs, gos, ubg, vecs,
        x, emb, row(ln1_gain), ghid,
    )
    return (
        out[None], tgrad[None], table, small[0], small[1], qkv.astype(f32).reshape(DC, 3, H), wo.astype(f32),
        small[2], small[3], small[4], ffn[0].astype(f32), small[7], ffn[1].astype(f32), small[5],
    )


def solution(mesh):
    R, C, Z = mesh.shape["row"], mesh.shape["col"], mesh.shape["dp"]
    batch = P(("dp", "col"), "row", None)
    block = P("col", "row")
    return jax.shard_map(
        functools.partial(body, R, C, Z),
        mesh=mesh,
        in_specs=(
            batch, batch, P(("dp", "col")), P(("dp", "col")), P("col", None), P(), P(), P("col", None, "row"), block,
            P(), P(), P(), block, P("row"), block, P(),
        ),
        out_specs=(
            batch, batch, P("col", None), P(), P(), P("col", None, "row"), block, P(), P(), P(), block, P("row"),
            block, P(),
        ),
        check_vma=False,
    )
```

time: 892 us -> 345 us (0.39)
  waiting for transfers between devices: 482 us -> 0 us
  Pallas kernels: 0 us -> 313 us
  matrix products: 196 us -> 0 us
  other arithmetic: 72.4 us -> 2.69 us
  blocking collectives: 62.7 us -> 0 us
  between operations: 16.4 us -> 2.09 us
  loops' own time: 14.1 us -> 0 us
  local copies, waits for them, and re-layouts: 33.4 us -> 22.9 us
    pallas_call x0 -> x3, Pallas kernels: none -> 313 us  [the longest x1 155 us: run_backward(): pl.pallas_call(functools.partial(backward_kernel, R, C, Z), out_shape=(sd...]
    dot_general x39 -> x0, matrix products: 190 us -> none  [the longest x8 31.4 us: one_block(): jnp.einsum('qhd,khd->hqk', query_blk, key_rows, preferred_element_type=jn...]
    reduce_scatter x5 -> x0, waiting for transfers between devices: 181 us -> none  [the longest x2 87.3 us: scatter_rows(): lax.psum_scatter(values.astype(jnp.bfloat16), 'row', scatter_dimension=1,...]
    all_gather x7 -> x0, waiting for transfers between devices: 177 us -> none  [the longest x2 84.9 us: gather_rows(): return lax.all_gather(values, 'row', axis=1, tiled=True)]
    psum x2 -> x0, waiting for transfers between devices: 119 us -> none  [the longest x1 67.2 us: body(): lax.psum(blocks[4].astype(jnp.bfloat16), ('dp', 'row')).astype(jnp.float32)]
    psum x2 -> x0, blocking collectives: 53.3 us -> none  [the longest x1 40.7 us: body(): lax.psum((ln1_gain_part, ln1_bias_part, jnp.sum(grad_hidden1, axis=(0, 1)...]
    reduce_sum x11 -> x0, other arithmetic: 43.4 us -> none  [the longest x4 27.1 us: one_block(): row_total = jnp.sum(exponent, axis=2, keepdims=True)]
    unnamed x93 -> x17, local copies, waits for them, and re-layouts: 23.4 us -> 8.29 us
  transfers between devices with their start and end apart: 18 -> 0, of which waited for: 15 -> 0; matrix products, arithmetic and copies ran while one was open for 20% -> 0% of each run, Pallas kernels for 0% -> 0%
where the time goes in v2:
time: 345 us; the launch traced here: 341 us
  Pallas kernels  313 us (91%)
  local copies, waits for them, and re-layouts  22.9 us (7%)
    pallas_call x1, Pallas kernels, run_backward(): pl.pallas_call(functools.partial(backward_kernel, R, C, Z), out_shape=(sd...  155 us
    pallas_call x1, Pallas kernels, run_forward(): pl.pallas_call(functools.partial(forward_kernel, R, C, Z), out_shape=(sds...  111 us
    pallas_call x1, Pallas kernels, run_middle(): pl.pallas_call(functools.partial(middle_kernel, R, C), out_shape=(sds((T,...  47.3 us
    broadcast_in_dim x7, local copies, waits for them, and re-layouts, body(): row = lambda vector: vector[None, :]  8.87 us
    unnamed x17, local copies, waits for them, and re-layouts  8.29 us

profile of v2, /device:TPU:15, one launch (start us, length us, event | category | flops | bytes accessed | tf_op | source)
XLA Modules:
  0.0 340.6 jit_solution(17783644076401461713)
XLA Ops:
  2.1 1.3 broadcast_in_dim.28.gain
  3.3 1.3 broadcast_in_dim.29.bias
  4.6 1.3 broadcast_in_dim.31.out_bias
  5.9 1.3 broadcast_in_dim.32.gain
  7.1 1.3 broadcast_in_dim.33.bias
  8.4 1.3 broadcast_in_dim.30.ub
  9.7 1.3 broadcast_in_dim.34.down_bias
  10.9 1.7 copy.35.wo
  12.6 2.0 copy.34.w
  14.6 0.0 copy-done.4
  14.6 1.1 pad_maximum_fusion.wud
  15.8 110.7 %forward_attention.1 = (bf16[3,2048,128]{2,1,0:T(8,128)(2,1)}, bf16[3,2048,128]{2,1,0:T(8,128)(2,1)}, bf16[3,2048,128]{2,1,0:T(8,128)(2,1)}, bf16[4,512,768]{2,1...) custom-call(s32[1]{0:T(128)S(6)} %copy.41.stamp, ...), custom_call_target="tpu_custom_call" | custom-call | tf_op jit(solution)/shard_map/forward_attention/pallas_call | solution.py:319
  126.4 47.3 %feed_forward.1 = (bf16[512,768]{1,0:T(8,128)(2,1)}, f32[512,768]{1,0:T(8,128)}, bf16[4,512,192]{2,1,0:T(8,128)(2,1)}, bf16[4,2,384,768]{3,2,1,0:T(8,128)(2,1)},...) custom-call(bf16[512,768]{1,0:T(8,128)(2,1)} %bitcast.15, bf16[512,768]{1,0:T(8,128)(2,1)} %bitcast.20, ...), custom_call_target="tpu_custom_call" | custom-call | tf_op jit(solution)/shard_map/feed_forward/pallas_call | solution.py:513
  173.8 154.9 %backward_attention.1 = (f32[512,768]{1,0:T(8,128)}, bf16[2,384,768]{2,1,0:T(8,128)(2,1)}, bf16[384,192]{1,0:T(8,128)(2,1)}, bf16[384,576]{1,0:T(8,128)(2,1)}, f32[8,768]{1,0:T(8,128)}, /*index=5*/f32[500,768]{1,0:T(8,128)}) custom-call(s32[1]{0:T(128)S(6)} %copy.41.stamp, s32[1]{0:T(128)S(6)} %copy.42.prefix_ref, ...), custom_call_target="tpu_custom_call" | custom-call | tf_op jit(solution)/shard_map/backward_attention/pallas_call | solution.py:825
  328.6 1.7 slice_reduce_fusion
  330.3 1.8 copy.37
  332.1 2.1 copy.36
  334.2 0.0 copy-done.2
  334.2 1.6 bitcast_convert_fusion
  335.8 0.9 copy.43
  336.7 0.8 copy-done
  337.5 1.1 copy.44
  338.6 0.8 copy-done.1
  339.4 1.1 copy.45
  (8 shorter events, 0.0 us)
Async XLA Ops:
  0.6 14.0 %copy-start.4 = (bf16[384,768]{1,0:T(8,128)(2,1)S(1)}, bf16[384,768]{1,0:T(8,128)(2,1)}, u32[]{:S(2)}) copy-start(bf16[384,768]{1,0:T(8,128)(2,1)} %param.30) | copy-start | bytes 1769476
  0.7 14.0 %copy-start.5 = (bf16[384,768]{1,0:T(8,128)(2,1)S(1)}, bf16[384,768]{1,0:T(8,128)(2,1)}, u32[]{:S(2)}) copy-start(bf16[384,768]{1,0:T(8,128)(2,1)} %param.28) | copy-start | bytes 1769476
  328.6 5.6 %copy-start.2 = (bf16[2,384,768]{2,1,0:T(8,128)(2,1)S(1)}, bf16[2,384,768]{2,1,0:T(8,128)(2,1)}, u32[]{:S(2)}) copy-start(bf16[2,384,768]{2,1,0:T(8,128)(2,1)} %get-tuple-element.61) | copy-start | bytes 3538948
  334.2 1.6 copy-start.3
  335.8 1.7 copy-start
  337.5 2.0 copy-start.1

commit v3 on v1

v3 whole, which is shorter than its diff:
```python
import functools
from types import SimpleNamespace

import jax
import jax.numpy as jnp
from jax import lax
from jax.experimental import pallas as pl
from jax.experimental.pallas import tpu as pltpu
from jax.sharding import PartitionSpec as P

HD = 64
LANES = 128
norm_eps = 1e-05
masked_score = -1e30
f32, bf16 = jnp.float32, jnp.bfloat16
MESH = pl.DeviceIdType.MESH
NN = (((1,), (0,)), ((), ()))
NT = (((1,), (1,)), ((), ()))
TN = (((0,), (0,)), ((), ()))
VM = pl.BlockSpec(memory_space=pltpu.VMEM)
SM = pl.BlockSpec(memory_space=pltpu.SMEM)
AN = pl.BlockSpec(memory_space=pl.ANY)
R = 4


def mm(a, b, dims):
    return lax.dot_general(a, b, dims, preferred_element_type=f32)


def remote(src, dst, sems, index, **where):
    return pltpu.make_async_remote_copy(
        src_ref=src, dst_ref=dst, send_sem=sems[0].at[index], recv_sem=sems[1].at[index],
        device_id=where, device_id_type=MESH,
    )


def flip(a, b):
    a0, b0, a1, b1 = lax.rem(a, 2), lax.rem(b, 2), a // 2, b // 2
    return a0 + b0 - 2 * a0 * b0 + 2 * (a1 + b1 - 2 * a1 * b1)


def greet(sizes):
    barrier = pltpu.get_barrier_semaphore()
    total = 0
    for name, count in sizes.items():
        for step in range(1, count):
            to = lax.rem(lax.axis_index(name) + step, count)
            pl.semaphore_signal(barrier, inc=1, device_id={name: to}, device_id_type=MESH)
            total += 1
    pl.semaphore_wait(barrier, total)


def normalize(hidden, width):
    average = jnp.sum(hidden, axis=-1, keepdims=True) / width
    variance = jnp.sum(hidden * hidden, axis=-1, keepdims=True) / width - average * average
    inverse = lax.rsqrt(variance + norm_eps)
    return (hidden - average) * inverse, inverse


def norm_back(grad, centred, inverse, gain, width):
    scaled = grad * gain
    first = jnp.sum(scaled, axis=-1, keepdims=True) / width
    second = jnp.sum(scaled * centred, axis=-1, keepdims=True) / width
    return inverse * (scaled - first - centred * second)


def split_parts(value, lane, count):
    out = jnp.zeros(lane.shape, f32)
    for place in range(count):
        high = value.astype(bf16).astype(f32)
        out = jnp.where(lane == place, high, out)
        value = value - high
    return out.astype(bf16)


def layer_kernel(names, C, Z, *refs):
    n = SimpleNamespace(**dict(zip([name for name in names if not name.startswith("sem_")], refs)))
    plain = sum(1 for name in names if not name.startswith("sem_"))
    sem = {}
    place = plain
    for name in names:
        if name.startswith("sem_"):
            sem[name[4:]] = (refs[place], refs[place + 1])
            place += 2
    local = refs[place]
    r, c, z = lax.axis_index("row"), lax.axis_index("col"), lax.axis_index("dp")
    T, D = n.x.shape
    DC, F = n.w_up.shape
    H = n.w_out.shape[1]
    heads = H // HD
    L = R * T
    half = T // 2
    NTB = n.table.shape[0]
    parity = lax.rem(z, 2)
    zpair = z + 1 - 2 * parity
    nx, ny = flip(r, 1), flip(r, 2)
    cols = pl.ds(pl.multiple_of(c * DC, DC), DC)
    vec = lambda row: n.vectors[row : row + 1, :]
    others = range(1, R)
    peers = range(1, C)
    groups = range(1, Z)

    def col_at(t):
        return lax.rem(c + t, C)

    def rows_of(device):
        return pl.ds(pl.multiple_of(device * DC, DC), DC)

    greet({"row": R, "col": C, "dp": Z})

    def stamp_copy(t):
        return remote(n.stamp_own, n.stamp_got.at[t - 1], sem["stamp"], t - 1, col=col_at(t))

    def pick_copy(t):
        return remote(n.picked.at[t - 1], n.picked_got.at[t - 1], sem["pick"], t - 1, col=lax.rem(c - t + C, C))

    def w_copy(t):
        return remote(n.w_qkv, n.wq.at[cols], sem["w"], t - 1, col=col_at(t))

    n.stamp_own[...] = jnp.full(n.stamp_own.shape, n.stamp[0].astype(f32))
    for t in peers:
        stamp_copy(t).start()
    for t in peers:
        w_copy(t).start()
    n.wq[cols, :] = n.w_qkv[...]

    def row_of(stamps):
        number = (lax.broadcasted_iota(jnp.int32, (NTB, D), 0) + c * NTB).astype(f32)
        return jnp.sum(jnp.where(number == stamps, n.table[...].astype(f32), 0.0), axis=0, keepdims=True)

    for t in peers:
        stamp_copy(t).wait_recv()
        n.picked[t - 1] = jnp.broadcast_to(row_of(n.stamp_got[t - 1][0:1, 0:1]), (8, D))
        pick_copy(t).start()
    embed = row_of(n.stamp_own[0:1, 0:1])
    for t in peers:
        pick_copy(t).wait_recv()
        embed = embed + n.picked_got[t - 1][0:1]
    n.emb[...] = jnp.broadcast_to(embed, n.emb.shape)

    def n_copy(link, part):
        piece = n.one.at[r, pl.ds(part * half, half)]
        return remote(piece, piece, sem["n"], 2 * link + part, row=(nx, ny)[link])

    def relay_copy(link):
        piece = n.one.at[(ny, nx)[link], pl.ds(link * half, half)]
        return remote(piece, piece, sem["relay"], link, row=(nx, ny)[link])

    rows_ln = 128
    for part in range(2):

        def norm_step(t, carry, part=part):
            rows = pl.ds(pl.multiple_of(part * half + t * rows_ln, rows_ln), rows_ln)
            centred, inverse = normalize(n.x[rows, :].astype(f32) + n.emb[0:1, :], D)
            n.one[r, rows, :] = (centred * vec(0) + vec(1)).astype(bf16)
            return carry

        lax.fori_loop(0, half // rows_ln, norm_step, 0)
        n_copy(1 - part, part).start()
    n_copy(0, 0).start()
    n_copy(1, 1).start()

    for t in peers:
        w_copy(t).wait_recv()
    lane = lax.broadcasted_iota(jnp.int32, (T, HD), 1)
    q_tail = jnp.zeros((T, HD), bf16)
    k_tail = jnp.where(lane < 3, 1.0, 0.0).astype(bf16)
    v_tail = jnp.where(lane < 2, 1.0, 0.0).astype(bf16)
    scale = HD ** (-0.5)

    def project(s, carry):
        @pl.when(s == 1)
        def _():
            n_copy(1, 0).wait_recv()
            relay_copy(0).start()
            n_copy(0, 1).wait_recv()
            relay_copy(1).start()
            n_copy(0, 0).wait_recv()

        @pl.when(s == 2)
        def _():
            n_copy(1, 1).wait_recv()

        @pl.when(s == 3)
        def _():
            relay_copy(0).wait_recv()
            relay_copy(1).wait_recv()
            weights_start()

        block = flip(r, s)
        y = mm(n.one[block], n.wq[...], NN).astype(bf16)
        rows = pl.ds(pl.multiple_of(block * T, T), T)
        for h in range(heads):
            n.q[h, rows, :] = jnp.concatenate([y[:, h * HD : (h + 1) * HD] * scale, q_tail], axis=1)
            n.k[h, rows, :] = jnp.concatenate([y[:, H + h * HD : H + (h + 1) * HD], k_tail], axis=1)
            n.v[h, rows, :] = jnp.concatenate([y[:, 2 * H + h * HD : 2 * H + (h + 1) * HD], v_tail], axis=1)
        return carry

    def up_down(kind, link, s, go):
        if s == 0:
            for t in peers:
                source = (n.w_up, n.w_down)[kind]
                go(remote(source, n.wud.at[kind, r, cols], sem["gc"], kind * (C - 1) + t - 1, col=col_at(t)))
            return
        source = (n.w_up, n.w_down)[kind]
        go(remote(source, n.wud.at[kind, r, cols], sem["g"], s - 1, row=flip(r, s)))

    def g_start(s):
        for kind in range(2):

            @pl.when(parity == kind)
            def _(kind=kind):
                up_down(kind, 0, s, lambda copy: copy.start())

    def g_copy(s):
        piece = n.wud.at[parity, flip(r, s), cols]
        return remote(n.w_up, piece, sem["g"], s - 1, row=flip(r, s))

    def z_copy(s):
        piece = n.wud.at[parity, flip(r, s), cols]
        return remote(piece, piece, sem["gz"], s - 1, dp=zpair)

    def gc_copy(s, kind, t):
        piece = n.wud.at[parity if kind == 0 else 1 - parity, flip(r, s), cols]
        return remote(piece, piece, sem["gc"], (2 * s + kind) * (C - 1) + t - 1, col=col_at(t))

    def gc_own(kind, t):
        source = (n.w_up, n.w_down)[kind]
        return remote(source, n.wud.at[kind, r, cols], sem["gc"], kind * (C - 1) + t - 1, col=col_at(t))

    def wo_copy(s):
        piece = n.wo.at[r, cols]
        return remote(n.w_out, piece, sem["wo"], s - 1, row=flip(r, s))

    def woc_copy(s, t):
        piece = n.wo.at[flip(r, s), cols]
        source = n.w_out if s == 0 else piece
        return remote(source, piece, sem["woc"], s * (C - 1) + t - 1, col=col_at(t))

    def ub_copy(s):
        return remote(n.ub.at[r], n.ub.at[r], sem["ub"], s - 1, row=flip(r, s))

    own_up = pltpu.make_async_copy(n.w_up, n.wud.at[0, r, cols], local.at[0])
    own_down = pltpu.make_async_copy(n.w_down, n.wud.at[1, r, cols], local.at[1])
    n.ub[r] = jnp.broadcast_to(n.vectors[6:7, 0:F], (8, F))
    n.wo[r, cols, :] = n.w_out[...]

    def weights_start():
        for s in others:
            wo_copy(s).start()
            ub_copy(s).start()
        g_start(1)
        g_start(2)

    for t in peers:
        woc_copy(0, t).start()
        for kind in range(2):
            gc_own(kind, t).start()
    own_up.start()
    own_down.start()

    lax.fori_loop(0, R, project, 0)

    prefix = n.prefix[0]
    longest = L // 2
    SB = min(256, T)
    nsub = T // SB
    lane_sb = lax.broadcasted_iota(jnp.int32, (SB, HD), 1)

    def a_copy(s):
        i = flip(r, s)
        return remote(n.mine.at[i], n.att.at[r], sem["a"], s - 1, row=i)

    def attend_block(step, carry):
        s = lax.rem(step + 1, R)
        i = flip(r, s)
        for static in range(R):
            early = (static + 1) * T <= longest
            nk = longest if early else (static + 1) * T
            nm = nk if early else T

            def attend(t, inner, nk=nk, nm=nm):
                h = t // nsub
                sub = pl.multiple_of(lax.rem(t, nsub) * SB, SB)
                row = i * T + sub
                rows = pl.ds(pl.multiple_of(row, SB), SB)
                scores = mm(n.q[h, rows, :], n.k[h, :nk, :], NT)
                limit = jnp.maximum(row + 1 + lax.broadcasted_iota(jnp.int32, (SB, 1), 0), prefix)
                key = (nk - nm) + lax.broadcasted_iota(jnp.int32, (SB, nm), 1)
                last = jnp.where(key < limit, scores[:, nk - nm :], masked_score)
                top = jnp.max(last, axis=1, keepdims=True)
                if nk > nm:
                    top = jnp.maximum(top, jnp.max(scores[:, : nk - nm], axis=1, keepdims=True))
                mixed = mm(jnp.exp(last - top).astype(bf16), n.v[h, nk - nm : nk, :], NN)
                if nk > nm:
                    mixed += mm(jnp.exp(scores[:, : nk - nm] - top).astype(bf16), n.v[h, : nk - nm, :], NN)
                weight = mixed[:, HD : HD + 1]
                n.mixed[h, pl.ds(sub, SB), :] = mixed / weight
                n.q[h, rows, HD:] = split_parts(-(top + jnp.log(weight)), lane_sb, 3)
                return inner

            @pl.when(i == static)
            def _(attend=attend):
                lax.fori_loop(0, heads * nsub, attend, 0)

        n.mine[i] = jnp.concatenate([n.mixed[h][:, :HD] for h in range(heads)], axis=1).astype(bf16)

        for at in range(R - 1):

            @pl.when(step == at)
            def _(at=at):
                a_copy(at + 1).start()
                if at == 0:
                    for s in others:
                        wo_copy(s).wait_recv()
                        for t in peers:
                            woc_copy(s, t).start()
                if at == 1:
                    for s in (1, 2):
                        g_copy(s).wait_recv()
                        z_copy(s).start()
                        for t in peers:
                            gc_copy(s, 0, t).start()
                    g_start(3)

        return carry

    def attend_all(mixed_ref):
        n.mixed = mixed_ref
        lax.fori_loop(0, R, attend_block, 0)

    pl.run_scoped(attend_all, pltpu.VMEM((heads, T, LANES), f32))
    n.att[r] = n.mine[r]

    TR = min(256, T)
    TF = 384 if F % 384 == 0 else F
    tiles = F // TF
    ticks = R * tiles

    def a2_copy(s):
        b = flip(r, s)
        return remote(n.gsend.at[b], n.gatt.at[r], sem["a2"], s - 1, row=b)

    def row_copy(s, kind):
        return remote(n.crecv.at[s, 0, kind], n.grow.at[s - 1, kind], sem["row"], 2 * (s - 1) + kind, row=flip(r, s))

    def wrow_copy(s):
        b = flip(r, s)
        return remote(n.orecv.at[0, b], n.orow.at[s - 1], sem["wrow"], s - 1, row=b)

    def u_copy(s):
        return remote(n.ubg.at[flip(r, s)], n.urow.at[s - 1], sem["u"], s - 1, row=flip(r, s))

    def middle(wbuf, acc, gn, n2, n2t, cott, gbuf, obuf):
        def fetch(tick):
            fcols = pl.ds(pl.multiple_of(lax.rem(tick, tiles) * TF, TF), TF)
            slot = lax.rem(tick, 2)
            return pltpu.make_async_copy(
                n.wud.at[:, flip(r, tick // tiles), :, fcols], wbuf.at[slot], local.at[2 + slot]
            )

        def c_copy(s, t):
            to = col_at(t)
            return remote(
                gbuf.at[lax.rem(s, 2), :, rows_of(to)], n.crecv.at[s, t - 1], sem["c"], s * (C - 1) + t - 1, col=to
            )

        def o_copy(t):
            to = col_at(t)
            return remote(obuf.at[:, rows_of(to)], n.orecv.at[t - 1], sem["o"], t - 1, col=to)

        def join(s):
            for t in peers:
                c_copy(s, t).wait_recv()
            for kind in range(2):
                total = gbuf[lax.rem(s, 2), kind, cols, :].astype(f32)
                for t in peers:
                    total = total + n.crecv[s, t - 1, kind].astype(f32)
                n.crecv[s, 0, kind] = total.astype(bf16)

        def send_row(s):
            u_copy(s).start()
            for kind in range(2):
                row_copy(s, kind).start()

        own_up.wait()
        own_down.wait()
        for t in peers:
            for kind in range(2):
                gc_own(kind, t).wait()
        fetch(0).start()
        cott[...] = n.cot[...].T
        for s in others:
            for t in peers:
                woc_copy(s, t).wait_recv()
        for t in peers:
            woc_copy(0, t).wait_recv()
        for s in others:
            ub_copy(s).wait_recv()
            a_copy(s).wait_recv()
        vsum = jnp.zeros((1, D), f32)
        for part in range(T // TR):
            rows = slice(part * TR, (part + 1) * TR)
            branch = mm(n.att[0, rows, :], n.wo[0], NT)
            for b in range(1, R):
                branch += mm(n.att[b, rows, :], n.wo[b], NT)
            hidden = n.x[rows, :].astype(f32) + n.emb[0:1, :] + branch + vec(2)
            n.tgrad[rows, :] = hidden
            centred, inverse = normalize(hidden, D)
            n2[rows, :] = (centred * vec(3) + vec(4)).astype(bf16)
            acc[rows, :] = jnp.zeros((TR, D), f32)
            gn[rows, :] = jnp.zeros((TR, D), f32)
            vsum = vsum + jnp.sum(n.cot[rows, :].astype(f32), axis=0, keepdims=True)
        n2t[...] = n2[...].T
        n.vbuf[5:6, :] = vsum

        def tick_step(tick, carry):
            s, t = tick // tiles, lax.rem(tick, tiles)
            b = flip(r, s)
            slot, wslot = lax.rem(s, 2), lax.rem(tick, 2)
            fetch(tick).wait()

            @pl.when((t == 0) & (s + 1 < R))
            def _():
                @pl.when(s == 0)
                def _():
                    g_copy(3).wait_recv()
                    z_copy(3).start()
                    for p in peers:
                        gc_copy(3, 0, p).start()

                z_copy(s + 1).wait_recv()
                for p in peers:
                    gc_copy(s + 1, 1, p).start()

            @pl.when((t == 0) & (s >= 2))
            def _():
                for p in peers:
                    c_copy(s - 2, p).wait_send()

            @pl.when((t == tiles - 1) & (s + 1 < R))
            def _():
                for p in peers:
                    gc_copy(s + 1, 0, p).wait_recv()
                    gc_copy(s + 1, 1, p).wait_recv()

            @pl.when(tick + 1 < ticks)
            def _():
                fetch(tick + 1).start()

            fcols = pl.ds(pl.multiple_of(t * TF, TF), TF)
            wu = wbuf[wslot, 0]
            wd = wbuf[wslot, 1]
            inner = mm(n2[...], wu, NN) + n.ub[b, 0:1, fcols]
            cdf = 0.5 * (1.0 + lax.erf(inner * 0.7071067811865476))
            slope = cdf + inner * (jnp.exp(-0.5 * inner * inner) * 0.3989422804014327)
            active = (inner * cdf).astype(bf16)
            acc[...] += mm(active, wd, NT)
            ginner = mm(n.cot[...], wd, NN) * slope
            glow = ginner.astype(bf16)
            gn[...] += mm(glow, wu, NT)
            gbuf[slot, 1, :, fcols] = mm(cott[...], active, NN).astype(bf16)
            gbuf[slot, 0, :, fcols] = mm(n2t[...], glow, NN).astype(bf16)
            n.ubg[b, :, fcols] = jnp.sum(ginner, axis=0, keepdims=True)

            @pl.when(t == tiles - 1)
            def _():
                for p in peers:
                    c_copy(s, p).start()

            @pl.when((t == 0) & (s > 0))
            def _():
                join(s - 1)

                @pl.when(s > 1)
                def _():
                    send_row(s - 1)

            return carry

        lax.fori_loop(0, ticks, tick_step, 0)

        gain_sum = jnp.zeros((1, D), f32)
        bias_sum = jnp.zeros((1, D), f32)
        hid_sum = jnp.zeros((1, D), f32)
        for part in range(T // TR):
            rows = slice(part * TR, (part + 1) * TR)
            hidden = n.tgrad[rows, :]
            n.out[rows, :] = (hidden + acc[rows, :] + vec(5)).astype(bf16)
            centred, inverse = normalize(hidden, D)
            g = gn[rows, :]
            gh = n.cot[rows, :].astype(f32) + norm_back(g, centred, inverse, vec(3), D)
            n.tgrad[rows, :] = gh
            n2[rows, :] = gh.astype(bf16)
            gain_sum = gain_sum + jnp.sum(g * centred, axis=0, keepdims=True)
            bias_sum = bias_sum + jnp.sum(g, axis=0, keepdims=True)
            hid_sum = hid_sum + jnp.sum(gh, axis=0, keepdims=True)
        n.vbuf[2:3, :] = hid_sum
        n.vbuf[3:4, :] = gain_sum
        n.vbuf[4:5, :] = bias_sum

        def back_step(at, carry):
            s = R - 1 - at
            b = flip(r, s)
            n.gsend[b] = mm(n2[...], n.wo[b], NN).astype(bf16)

            @pl.when(s > 0)
            def _():
                a2_copy(s).start()

            return carry

        lax.fori_loop(0, R, back_step, 0)
        n.gatt[r] = n.gsend[r]
        n2t[...] = n2[...].T
        join(R - 1)
        send_row(R - 1)

        def out_step(b, carry):
            obuf[b] = mm(n2t[...], n.att[b], NN).astype(bf16)
            return carry

        lax.fori_loop(0, R, out_step, 0)
        for t in peers:
            o_copy(t).start()
        for t in peers:
            o_copy(t).wait_recv()
        for b in range(R):
            total = obuf[b, cols, :].astype(f32)
            for t in peers:
                total = total + n.orecv[t - 1, b].astype(f32)
            n.orecv[0, b] = total.astype(bf16)
        for s in others:
            wrow_copy(s).start()
        for t in peers:
            o_copy(t).wait_send()
            for s in range(R - 2, R):
                c_copy(s, t).wait_send()

    dt = bf16
    pl.run_scoped(
        middle,
        pltpu.VMEM((2, 2, D, TF), dt), pltpu.VMEM((T, D), f32), pltpu.VMEM((T, D), f32), pltpu.VMEM((T, D), dt),
        pltpu.VMEM((D, T), dt), pltpu.VMEM((D, T), dt), pltpu.VMEM((2, 2, D, F), dt), pltpu.VMEM((R, D, H), dt),
    )

    DZ = n.zr.shape[2]
    split = DZ != DC
    sources = (n.crecv.at[0, 0, 0], n.crecv.at[0, 0, 1], n.oblk, n.qblk)
    landing = (n.zr.at[0], n.zr.at[1], n.zro, n.zrq)
    finals = (n.up_out, n.down_out, n.wo_out, n.qkv_out)

    def part_of(device):
        return pl.ds(pl.multiple_of(device * DZ, DZ), DZ) if split else slice(None)

    def zz_copy(kind, s):
        to = lax.rem(z + s, Z)
        return remote(sources[kind].at[part_of(to)], landing[kind].at[s - 1], sem["z"], kind * (Z - 1) + s - 1, dp=to)

    def y_copy(kind, s):
        piece = finals[kind].at[part_of(z)]
        return remote(piece, piece, sem["y"], kind * (Z - 1) + s - 1, dp=lax.rem(z + s, Z))

    def row_sum(kind):
        for s in others:
            row_copy(s, kind).wait_recv()
        total = n.crecv[0, 0, kind].astype(f32)
        for s in others:
            total = total + n.grow[s - 1, kind].astype(f32)
        n.crecv[0, 0, kind] = total.astype(bf16)
        for s in groups:
            zz_copy(kind, s).start()

    def wrow_sum():
        for s in others:
            wrow_copy(s).wait_recv()
        total = n.orecv[0, r].astype(f32)
        for s in others:
            total = total + n.orow[s - 1].astype(f32)
        n.oblk[...] = total.astype(bf16)
        for s in groups:
            zz_copy(2, s).start()

    def data_sum(kind):
        for s in groups:
            zz_copy(kind, s).wait_recv()
        total = sources[kind][part_of(z), :].astype(f32)
        for s in groups:
            total = total + landing[kind][s - 1].astype(f32)
        finals[kind][part_of(z), :] = total.astype(bf16)
        if split:
            for s in groups:
                y_copy(kind, s).start()

    def p_copy(link, part, b):
        piece = pl.ds(part * half, half)
        return remote(n.part.at[b, piece], n.prec.at[link, piece], sem["p"], 2 * link + part, row=(nx, ny)[link])

    def pr_copy(link, b):
        return remote(n.part.at[b, pl.ds(link * half, half)], n.prel.at[link], sem["pr"], link, row=(nx, ny)[link])

    def back(d, dq, dk, dv, gp, qg):
        def spread(b):
            rows = pl.ds(b * T, T)

            @pl.when(r != b)
            def _():
                s = flip(r, b)
                remote(n.gsend.at[b], n.gatt.at[b], sem["a2"], s - 1, row=b).wait_recv()

            ga = n.gatt[b]
            both = ga.astype(f32) * n.mine[b].astype(f32)
            for h in range(heads):
                piece = slice(h * HD, (h + 1) * HD)
                delta = jnp.sum(both[:, piece], axis=1, keepdims=True)
                d[h, rows, :] = jnp.concatenate([ga[:, piece], split_parts(-delta, lane, 2)], axis=1)

        def pair(h, i, j, masked):
            qs = pl.ds(pl.multiple_of(i * T, T), T)
            ks = pl.ds(pl.multiple_of(j * T, T), T)
            qb, kb, vb, db = n.q[h, qs, :], n.k[h, ks, :], n.v[h, ks, :], d[h, qs, :]
            scores = mm(kb, qb, NT)
            if masked:
                limit = jnp.maximum(i * T + 1 + lax.broadcasted_iota(jnp.int32, (1, T), 1), prefix)
                key = j * T + lax.broadcasted_iota(jnp.int32, (T, T), 0)
                scores = jnp.where(key < limit, scores, masked_score)
            probs = jnp.exp(scores)
            gscores = (probs * mm(vb, db, NT)).astype(bf16)
            dv[h, ks, :] += mm(probs.astype(bf16), db, NN)
            dk[h, ks, :] += mm(gscores, qb, NN)
            dq[h, qs, :] += mm(gscores, kb, TN)

        def finish(b):
            rows = pl.ds(b * T, T)
            stack = jnp.concatenate(
                [dq[h, rows, :][:, :HD] * scale for h in range(heads)]
                + [dk[h, rows, :][:, :HD] for h in range(heads)]
                + [dv[h, rows, :][:, :HD] for h in range(heads)],
                axis=1,
            ).astype(bf16)
            gp[b] = stack
            n.part[b] = mm(stack, n.wq[...], NT).astype(bf16)
            s = flip(r, b)

            @pl.when(s == 3)
            def _():
                pr_copy(0, b).start()
                pr_copy(1, b).start()

            for link in range(2):

                @pl.when(s == link + 1)
                def _(link=link):
                    p_copy(link, link, b).start()

        def combine(b):
            s = flip(r, b)
            for link in range(2):

                @pl.when(s == link + 1)
                def _(link=link):
                    came = 1 - link
                    pr_copy(came, b).wait_recv()
                    piece = pl.ds(came * half, half)
                    total = n.part[b, piece, :].astype(f32) + n.prel[came].astype(f32)
                    n.part[b, piece, :] = total.astype(bf16)
                    p_copy(link, came, b).start()

        dq[...] = jnp.zeros_like(dq)
        dk[...] = jnp.zeros_like(dk)
        dv[...] = jnp.zeros_like(dv)
        early = R // 2
        for i in range(R - 1, early - 1, -1):
            spread(i)

            def plain_pair(t, carry, i=i):
                pair(t // i, i, lax.rem(t, i), False)
                return carry

            def diagonal(h, carry, i=i):
                pair(h, i, i, True)
                return carry

            lax.fori_loop(0, heads * i, plain_pair, 0)
            lax.fori_loop(0, heads, diagonal, 0)
            finish(i)
            if i + 1 < R:
                combine(i + 1)
        for i in range(early - 1, -1, -1):
            spread(i)
        row_sum(0)

        def square(t, carry):
            rest = lax.rem(t, early * early)
            pair(t // (early * early), rest // early, lax.rem(rest, early), True)
            return carry

        lax.fori_loop(0, heads * early * early, square, 0)
        for b in range(early - 1, -1, -1):
            finish(b)
        combine(early)
        row_sum(1)
        wrow_sum()

        qg[...] = jnp.zeros_like(qg)

        def qkv_step(b, carry):
            qg[...] += mm(n.one[b], gp[b], TN)
            return carry

        lax.fori_loop(0, R, qkv_step, 0)
        n.qgb[...] = qg[...].astype(bf16)

        def q_copy(t):
            to = col_at(t)
            return remote(n.qgb.at[rows_of(to)], n.qrecv.at[t - 1], sem["q"], t - 1, col=to)

        for t in peers:
            q_copy(t).start()
        for b in range(early - 1, -1, -1):
            combine(b)
        data_sum(0)
        for t in peers:
            q_copy(t).wait()
        total = n.qgb[cols, :].astype(f32)
        for t in peers:
            total = total + n.qrecv[t - 1].astype(f32)
        n.qblk[...] = total.astype(bf16)
        for s in groups:
            zz_copy(3, s).start()

    pl.run_scoped(
        back,
        pltpu.VMEM((heads, L, LANES), bf16), pltpu.VMEM((heads, L, LANES), f32), pltpu.VMEM((heads, L, LANES), f32),
        pltpu.VMEM((heads, L, LANES), f32), pltpu.VMEM((R, T, 3 * H), bf16), pltpu.VMEM((D, 3 * H), f32),
    )
    data_sum(1)
    data_sum(2)

    for link in range(2):
        for part in range(2):
            p_copy(link, part, 0).wait_recv()
    gain_sum = jnp.zeros((1, D), f32)
    bias_sum = jnp.zeros((1, D), f32)
    all_sum = jnp.zeros((1, D), f32)
    for piece in range(T // TR):
        rows = slice(piece * TR, (piece + 1) * TR)
        g = n.part[r, rows, :].astype(f32) + n.prec[0, rows, :].astype(f32) + n.prec[1, rows, :].astype(f32)
        centred, inverse = normalize(n.x[rows, :].astype(f32) + n.emb[0:1, :], D)
        total = n.tgrad[rows, :] + norm_back(g, centred, inverse, vec(0), D)
        n.tgrad[rows, :] = total
        gain_sum = gain_sum + jnp.sum(g * centred, axis=0, keepdims=True)
        bias_sum = bias_sum + jnp.sum(g, axis=0, keepdims=True)
        all_sum = all_sum + jnp.sum(total, axis=0, keepdims=True)

    n.vbuf[0:1, :] = gain_sum
    n.vbuf[1:2, :] = bias_sum
    n.vbuf[6:7, :] = all_sum
    n.vbuf[7:8, :] = jnp.zeros((1, D), f32)

    def v_copy(s):
        return remote(n.vbuf, n.vrow.at[s - 1], sem["v"], s - 1, row=flip(r, s))

    def vc_copy(t):
        return remote(n.vcol.at[c], n.vcol.at[c], sem["vc"], t - 1, col=col_at(t))

    def vz_copy(s):
        return remote(n.vcol, n.vz.at[s - 1], sem["vz"], s - 1, dp=lax.rem(z + s, Z))

    for s in others:
        v_copy(s).start()
    up_bias = n.ubg[r]
    for s in others:
        u_copy(s).wait_recv()
        up_bias = up_bias + n.urow[s - 1]
    for s in others:
        v_copy(s).wait_recv()
    total = n.vbuf[...]
    for s in others:
        total = total + n.vrow[s - 1]
    n.vcol[c, 0:8, :] = total
    n.vcol[c, 7:8, :] = up_bias
    n.vcol[c, 8:16, :] = jnp.full((8, D), n.stamp[0].astype(f32))
    for t in peers:
        vc_copy(t).start()
    for t in peers:
        vc_copy(t).wait_recv()
    for s in groups:
        vz_copy(s).start()
    data_sum(3)
    for s in groups:
        vz_copy(s).wait_recv()
    total = jnp.zeros((8, D), f32)
    number = (lax.broadcasted_iota(jnp.int32, (NTB, D), 0) + c * NTB).astype(f32)
    table = jnp.zeros((NTB, D), f32)
    for s in range(Z):
        for t in range(C):
            entry = n.vcol[t] if s == 0 else n.vz[s - 1, t]
            total = total + entry[0:8]
            table = table + jnp.where(number == entry[8:9], entry[6:7], 0.0)
    n.small[...] = total
    n.table_out[...] = table

    for t in peers:
        stamp_copy(t).wait_send()
        pick_copy(t).wait_send()
        w_copy(t).wait_send()
        vc_copy(t).wait_send()
        for s in range(R):
            woc_copy(s, t).wait_send()
            if s > 0:
                gc_copy(s, 0, t).wait_send()
                gc_copy(s, 1, t).wait_send()
    for link in range(2):
        relay_copy(link).wait_send()
        pr_copy(link, 0).wait_send()
        for part in range(2):
            n_copy(link, part).wait_send()
            p_copy(link, part, 0).wait_send()
    for s in others:
        for copy in (a_copy, g_copy, z_copy, wo_copy, ub_copy, a2_copy, wrow_copy, u_copy, v_copy):
            copy(s).wait_send()
        for kind in range(2):
            row_copy(s, kind).wait_send()
    for s in groups:
        vz_copy(s).wait_send()
        for kind in range(4):
            zz_copy(kind, s).wait_send()
            if split:
                y_copy(kind, s).wait()


def run_layer(C, Z, stamp, prefix, x, cot, table, vectors, w_qkv, w_out, w_up, w_down):
    T, D = x.shape
    DC, F = w_up.shape
    H = w_out.shape[1]
    heads = H // HD
    L = R * T
    NTB = table.shape[0]
    DZ = DC // Z if DC % (16 * Z) == 0 else DC
    vm = pltpu.VMEM
    ins = dict(stamp=SM, prefix=SM, x=VM, cot=VM, table=VM, vectors=VM, w_qkv=VM, w_out=VM, w_up=AN, w_down=AN)
    outs = dict(
        out=((T, D), bf16), tgrad=((T, D), f32), up_out=((DC, F), bf16), down_out=((DC, F), bf16),
        wo_out=((DC, H), bf16), qkv_out=((DC, 3 * H), bf16), small=((8, D), f32), table_out=((NTB, D), f32),
        wud=((2, R, D, F), bf16),
    )
    scratch = dict(
        stamp_own=vm((8, LANES), f32), stamp_got=vm((C - 1, 8, LANES), f32), picked=vm((C - 1, 8, D), f32),
        picked_got=vm((C - 1, 8, D), f32), emb=vm((8, D), f32), wq=vm((D, 3 * H), bf16), one=vm((R, T, D), bf16),
        q=vm((heads, L, LANES), bf16), k=vm((heads, L, LANES), bf16), v=vm((heads, L, LANES), bf16),
        mine=vm((R, T, H), bf16), att=vm((R, T, H), bf16), wo=vm((R, D, H), bf16),
        ub=vm((R, 8, F), f32), vbuf=vm((8, D), f32), ubg=vm((R, 1, F), f32),
        crecv=vm((R, C - 1, 2, DC, F), bf16), orecv=vm((C - 1, R, DC, H), bf16), gsend=vm((R, T, H), bf16),
        gatt=vm((R, T, H), bf16), grow=vm((R - 1, 2, DC, F), bf16), orow=vm((R - 1, DC, H), bf16),
        urow=vm((R - 1, 1, F), f32), part=vm((R, T, D), bf16), prec=vm((2, T, D), bf16), prel=vm((2, T // 2, D), bf16),
        qgb=vm((D, 3 * H), bf16), qrecv=vm((C - 1, DC, 3 * H), bf16), oblk=vm((DC, H), bf16), qblk=vm((DC, 3 * H), bf16),
        zr=vm((2, Z - 1, DZ, F), bf16), zro=vm((Z - 1, DZ, H), bf16), zrq=vm((Z - 1, DZ, 3 * H), bf16),
        vrow=vm((R - 1, 8, D), f32), vcol=vm((C, 16, D), f32), vz=vm((Z - 1, C, 16, D), f32),
    )
    sems = dict(
        stamp=C - 1, pick=C - 1, w=C - 1, n=4, relay=2, g=R - 1, gz=R - 1, gc=2 * R * (C - 1), wo=R - 1,
        woc=R * (C - 1), ub=R - 1, a=R - 1, a2=R - 1, row=2 * (R - 1), wrow=R - 1, u=R - 1, c=R * (C - 1), o=C - 1,
        z=4 * (Z - 1), y=4 * (Z - 1), p=4, pr=2, q=C - 1, v=R - 1, vc=C - 1, vz=Z - 1,
    )
    names = list(ins) + list(outs) + list(scratch) + ["sem_" + name for name in sems]
    dma = pltpu.SemaphoreType.DMA
    semaphores = []
    for count in sems.values():
        semaphores += [dma((count,)), dma((count,))]
    results = pl.pallas_call(
        functools.partial(layer_kernel, names, C, Z),
        out_shape=tuple(jax.ShapeDtypeStruct(*spec) for spec in outs.values()),
        in_specs=list(ins.values()),
        out_specs=(VM,) * (len(outs) - 1) + (AN,),
        scratch_shapes=list(scratch.values()) + semaphores + [dma((4,))],
        compiler_params=pltpu.CompilerParams(collective_id=0, has_side_effects=True, vmem_limit_bytes=67043328),
        name="layer",
    )(stamp, prefix, x, cot, table, vectors, w_qkv, w_out, w_up, w_down)
    return dict(zip(outs, results))


def body(C, Z, *args):
    (tokens, cotangent, timesteps, prefix_len, time_table, ln1_gain, ln1_bias, w_qkv, w_out, out_bias,
     ln2_gain, ln2_bias, w_up, up_bias, w_down, down_bias) = args
    DC, _, H = w_qkv.shape
    vectors = jnp.stack([ln1_gain, ln1_bias, out_bias, ln2_gain, ln2_bias, down_bias, up_bias, up_bias])
    o = run_layer(
        C, Z, timesteps, prefix_len, tokens[0], cotangent[0], time_table, vectors, w_qkv.reshape(DC, 3 * H), w_out,
        w_up, w_down,
    )
    small = o["small"]
    return (
        o["out"][None], o["tgrad"][None], o["table_out"], small[0], small[1],
        o["qkv_out"].astype(f32).reshape(DC, 3, H), o["wo_out"].astype(f32), small[2], small[3], small[4],
        o["up_out"].astype(f32), small[7], o["down_out"].astype(f32), small[5],
    )


def solution(mesh):
    C, Z = mesh.shape["col"], mesh.shape["dp"]
    batch = P(("dp", "col"), "row", None)
    block = P("col", "row")
    return jax.shard_map(
        functools.partial(body, C, Z),
        mesh=mesh,
        in_specs=(
            batch, batch, P(("dp", "col")), P(("dp", "col")), P("col", None), P(), P(), P("col", None, "row"), block,
            P(), P(), P(), block, P("row"), block, P(),
        ),
        out_specs=(
            batch, batch, P("col", None), P(), P(), P("col", None, "row"), block, P(), P(), P(), block, P("row"),
            block, P(),
        ),
        check_vma=False,
    )
```

time: 892 us -> 315 us (0.35)
  the two profiles are of different devices: /device:TPU:15 before, /device:TPU:26 now
where the time goes in v3:
time: 315 us; the launch traced here: 314 us
  Pallas kernels  291 us (92%)
  local copies, waits for them, and re-layouts  19 us (6%)
    pallas_call x1, Pallas kernels, run_layer(): pl.pallas_call(functools.partial(layer_kernel, names, C, Z), out_shape=tu...  291 us
    unnamed x15, local copies, waits for them, and re-layouts  7.48 us

profile of v3, /device:TPU:26, one launch (start us, length us, event | category | flops | bytes accessed | tf_op | source)
XLA Modules:
  0.0 314.0 jit_solution(4991160530367778669)
XLA Ops:
  1.9 0.7 stack.25
  2.6 0.7 stack.26
  3.3 0.7 stack.27
  4.0 0.7 stack.28
  4.7 0.7 stack.29
  5.4 0.7 stack.31
  6.1 0.7 stack.30
  6.8 0.6 stack.32.refs_5_
  7.4 1.7 copy.35.refs_7_
  9.1 2.0 copy.34.refs_6_
  11.1 290.8 %layer.1 = (bf16[512,768]{1,0:T(8,128)(2,1)}, f32[512,768]{1,0:T(8,128)}, bf16[384,768]{1,0:T(8,128)(2,1)}, bf16[384,768]{1,0:T(8,128)(2,1)}, bf16[384,192]{1,0:...) custom-call(s32[1]{0:T(128)S(6)} %copy.41.refs_0_, ...), custom_call_target="tpu_custom_call" | custom-call | tf_op jit(solution)/shard_map/layer/pallas_call | solution.py:871
  302.0 0.0 copy-start.4
  302.0 1.8 slice_reduce_fusion
  303.8 1.8 copy.37
  305.6 2.2 copy.36
  307.8 0.0 copy-done.4
  307.8 1.1 convert_element_type.11
  308.9 0.0 copy-done.3
  308.9 1.1 convert_element_type.12
  310.0 0.0 copy-done.2
  310.0 0.9 copy.43
  310.9 1.1 copy.44
  312.0 0.8 copy-done.1
  312.8 1.1 copy.45
  (5 shorter events, 0.0 us)
Async XLA Ops:
  302.0 5.8 %copy-start.4 = (bf16[384,768]{1,0:T(8,128)(2,1)S(1)}, bf16[384,768]{1,0:T(8,128)(2,1)}, u32[]{:S(2)}) copy-start(bf16[384,768]{1,0:T(8,128)(2,1)} %get-tuple-element.28) | copy-start | bytes 1769476
  305.6 3.3 %copy-start.3 = (bf16[384,768]{1,0:T(8,128)(2,1)S(1)}, bf16[384,768]{1,0:T(8,128)(2,1)}, u32[]{:S(2)}) copy-start(bf16[384,768]{1,0:T(8,128)(2,1)} %get-tuple-element.29) | copy-start | bytes 1769476
  307.8 2.2 copy-start.2
  308.9 2.0 copy-start
  310.9 2.0 copy-start.1

commit v4 on v3

--- a/solution.py
+++ b/solution.py
@@ -47,6 +47,11 @@
             to = lax.rem(lax.axis_index(name) + step, count)
             pl.semaphore_signal(barrier, inc=1, device_id={name: to}, device_id_type=MESH)
             total += 1
+    for s in range(1, sizes["dp"]):
+        for t in range(1, sizes["col"]):
+            to = {"dp": lax.rem(lax.axis_index("dp") + s, sizes["dp"]), "col": lax.rem(lax.axis_index("col") + t, sizes["col"])}
+            pl.semaphore_signal(barrier, inc=1, device_id=to, device_id_type=MESH)
+            total += 1
     pl.semaphore_wait(barrier, total)
 
 
@@ -86,7 +91,7 @@
     r, c, z = lax.axis_index("row"), lax.axis_index("col"), lax.axis_index("dp")
     T, D = n.x.shape
     DC, F = n.w_up.shape
-    H = n.w_out.shape[1]
+    H = n.w_out.shape[0]
     heads = H // HD
     L = R * T
     half = T // 2
@@ -96,6 +101,9 @@
     nx, ny = flip(r, 1), flip(r, 2)
     cols = pl.ds(pl.multiple_of(c * DC, DC), DC)
     vec = lambda row: n.vectors[row : row + 1, :]
+    given = (n.ln1_gain, n.ln1_bias, n.out_bias, n.ln2_gain, n.ln2_bias, n.down_bias, n.up_bias)
+    for row, ref in enumerate(given):
+        n.vectors[row : row + 1, :] = ref[...].reshape(1, D)
     others = range(1, R)
     peers = range(1, C)
     groups = range(1, Z)
@@ -103,11 +111,34 @@
     def col_at(t):
         return lax.rem(c + t, C)
 
+    def lanes(value, device):
+        return value[:, device * DC : (device + 1) * DC]
+
     def rows_of(device):
         return pl.ds(pl.multiple_of(device * DC, DC), DC)
 
     greet({"row": R, "col": C, "dp": Z})
 
+    def wo_copy(s):
+        piece = n.wo.at[r, c]
+        return remote(n.w_out, piece, sem["wo"], s - 1, row=flip(r, s))
+
+    def woc_copy(s, t):
+        piece = n.wo.at[flip(r, s), c]
+        source = n.w_out if s == 0 else piece
+        return remote(source, piece, sem["woc"], s * (C - 1) + t - 1, col=col_at(t))
+
+    def ub_copy(s):
+        return remote(n.ub.at[r], n.ub.at[r], sem["ub"], s - 1, row=flip(r, s))
+
+    n.ub[r] = jnp.broadcast_to(vec(6), (8, F))
+    n.wo[r, c] = n.w_out[...]
+    for s in others:
+        wo_copy(s).start()
+        ub_copy(s).start()
+    for t in peers:
+        woc_copy(0, t).start()
+
     def stamp_copy(t):
         return remote(n.stamp_own, n.stamp_got.at[t - 1], sem["stamp"], t - 1, col=col_at(t))
 
@@ -115,14 +146,14 @@
         return remote(n.picked.at[t - 1], n.picked_got.at[t - 1], sem["pick"], t - 1, col=lax.rem(c - t + C, C))
 
     def w_copy(t):
-        return remote(n.w_qkv, n.wq.at[cols], sem["w"], t - 1, col=col_at(t))
+        return remote(n.w_qkv, n.wq.at[c], sem["w"], t - 1, col=col_at(t))
 
     n.stamp_own[...] = jnp.full(n.stamp_own.shape, n.stamp[0].astype(f32))
     for t in peers:
         stamp_copy(t).start()
     for t in peers:
         w_copy(t).start()
-    n.wq[cols, :] = n.w_qkv[...]
+    n.wq[c] = n.w_qkv[...]
 
     def row_of(stamps):
         number = (lax.broadcasted_iota(jnp.int32, (NTB, D), 0) + c * NTB).astype(f32)
@@ -188,7 +219,11 @@
             weights_start()
 
         block = flip(r, s)
-        y = mm(n.one[block], n.wq[...], NN).astype(bf16)
+        normed = n.one[block]
+        y = mm(lanes(normed, 0), n.wq[0], NT)
+        for device in range(1, C):
+            y += mm(lanes(normed, device), n.wq[device], NT)
+        y = y.astype(bf16)
         rows = pl.ds(pl.multiple_of(block * T, T), T)
         for h in range(heads):
             n.q[h, rows, :] = jnp.concatenate([y[:, h * HD : (h + 1) * HD] * scale, q_tail], axis=1)
@@ -196,68 +231,43 @@
             n.v[h, rows, :] = jnp.concatenate([y[:, 2 * H + h * HD : 2 * H + (h + 1) * HD], v_tail], axis=1)
         return carry
 
-    def up_down(kind, link, s, go):
-        if s == 0:
-            for t in peers:
-                source = (n.w_up, n.w_down)[kind]
-                go(remote(source, n.wud.at[kind, r, cols], sem["gc"], kind * (C - 1) + t - 1, col=col_at(t)))
-            return
-        source = (n.w_up, n.w_down)[kind]
-        go(remote(source, n.wud.at[kind, r, cols], sem["g"], s - 1, row=flip(r, s)))
-
-    def g_start(s):
-        for kind in range(2):
-
-            @pl.when(parity == kind)
-            def _(kind=kind):
-                up_down(kind, 0, s, lambda copy: copy.start())
-
-    def g_copy(s):
-        piece = n.wud.at[parity, flip(r, s), cols]
-        return remote(n.w_up, piece, sem["g"], s - 1, row=flip(r, s))
+    ups = (n.w_up, n.w_down)
+
+    def half_copy(s, kind):
+        return remote(ups[kind], n.wud.at[kind, r, cols], sem["g"], s - 1, row=flip(r, s))
 
     def z_copy(s):
         piece = n.wud.at[parity, flip(r, s), cols]
         return remote(piece, piece, sem["gz"], s - 1, dp=zpair)
 
     def gc_copy(s, kind, t):
-        piece = n.wud.at[parity if kind == 0 else 1 - parity, flip(r, s), cols]
-        return remote(piece, piece, sem["gc"], (2 * s + kind) * (C - 1) + t - 1, col=col_at(t))
-
-    def gc_own(kind, t):
-        source = (n.w_up, n.w_down)[kind]
-        return remote(source, n.wud.at[kind, r, cols], sem["gc"], kind * (C - 1) + t - 1, col=col_at(t))
-
-    def wo_copy(s):
-        piece = n.wo.at[r, cols]
-        return remote(n.w_out, piece, sem["wo"], s - 1, row=flip(r, s))
-
-    def woc_copy(s, t):
-        piece = n.wo.at[flip(r, s), cols]
-        source = n.w_out if s == 0 else piece
-        return remote(source, piece, sem["woc"], s * (C - 1) + t - 1, col=col_at(t))
-
-    def ub_copy(s):
-        return remote(n.ub.at[r], n.ub.at[r], sem["ub"], s - 1, row=flip(r, s))
-
-    own_up = pltpu.make_async_copy(n.w_up, n.wud.at[0, r, cols], local.at[0])
-    own_down = pltpu.make_async_copy(n.w_down, n.wud.at[1, r, cols], local.at[1])
-    n.ub[r] = jnp.broadcast_to(n.vectors[6:7, 0:F], (8, F))
-    n.wo[r, cols, :] = n.w_out[...]
+        piece = n.wud.at[kind, flip(r, s), cols]
+        source = ups[kind] if s == 0 else piece
+        return remote(source, piece, sem["gc"], (2 * s + kind) * (C - 1) + t - 1, col=col_at(t))
+
+    def gc_half(s, second, t):
+        piece = n.wud.at[1 - parity if second else parity, flip(r, s), cols]
+        return remote(piece, piece, sem["gc"], (2 * s + second) * (C - 1) + t - 1, col=col_at(t))
+
+    def half_start(s):
+        for kind in range(2):
+
+            @pl.when(parity == kind)
+            def _(kind=kind):
+                half_copy(s, kind).start()
+
+    def half_on(s):
+        half_copy(s, 0).wait_recv()
+        z_copy(s).start()
+        for t in peers:
+            gc_half(s, 0, t).start()
 
     def weights_start():
-        for s in others:
-            wo_copy(s).start()
-            ub_copy(s).start()
-        g_start(1)
-        g_start(2)
+        half_start(3)
 
     for t in peers:
-        woc_copy(0, t).start()
         for kind in range(2):
-            gc_own(kind, t).start()
-    own_up.start()
-    own_down.start()
+            gc_copy(0, kind, t).start()
 
     lax.fori_loop(0, R, project, 0)
 
@@ -315,13 +325,10 @@
                         wo_copy(s).wait_recv()
                         for t in peers:
                             woc_copy(s, t).start()
-                if at == 1:
-                    for s in (1, 2):
-                        g_copy(s).wait_recv()
-                        z_copy(s).start()
-                        for t in peers:
-                            gc_copy(s, 0, t).start()
-                    g_start(3)
+                    half_start(1)
+                    half_start(2)
+                if at == 2:
+                    half_on(3)
 
         return carry
 
@@ -331,18 +338,48 @@
 
     pl.run_scoped(attend_all, pltpu.VMEM((heads, T, LANES), f32))
     n.att[r] = n.mine[r]
+    half_on(1)
 
     TR = min(256, T)
     TF = 384 if F % 384 == 0 else F
     tiles = F // TF
     ticks = R * tiles
 
+    def turn(k):
+        return lax.rem(156 // ((1 + 3 * lax.rem(k, 2)) * (1 + 15 * (k // 2))), R)
+
     def a2_copy(s):
         b = flip(r, s)
         return remote(n.gsend.at[b], n.gatt.at[r], sem["a2"], s - 1, row=b)
 
+    z_first = n.grow.shape[1] == 1
+    row_kinds = (0,) if z_first else (0, 1)
+
     def row_copy(s, kind):
         return remote(n.crecv.at[s, 0, kind], n.grow.at[s - 1, kind], sem["row"], 2 * (s - 1) + kind, row=flip(r, s))
+
+    def b_part(device):
+        height = n.bsum.shape[1]
+        return pl.ds(pl.multiple_of(device * height, height), height)
+
+    def b_copy(s, g):
+        to = lax.rem(z + g, Z)
+        return remote(n.crecv.at[s, 0, 1, b_part(to)], n.bz.at[s, g - 1], sem["b"], s * (Z - 1) + g - 1, dp=to)
+
+    def br_copy(s):
+        return remote(n.bsum.at[s], n.brow.at[s - 1], sem["br"], s - 1, row=flip(r, s))
+
+    def b_sum(s):
+        if not z_first:
+            return
+        for g in groups:
+            b_copy(s, g).wait_recv()
+        total = n.crecv[s, 0, 1, b_part(z), :].astype(f32)
+        for g in groups:
+            total = total + n.bz[s, g - 1].astype(f32)
+        n.bsum[s] = total.astype(bf16)
+        if s > 0:
+            br_copy(s).start()
 
     def wrow_copy(s):
         b = flip(r, s)
@@ -356,39 +393,64 @@
             fcols = pl.ds(pl.multiple_of(lax.rem(tick, tiles) * TF, TF), TF)
             slot = lax.rem(tick, 2)
             return pltpu.make_async_copy(
-                n.wud.at[:, flip(r, tick // tiles), :, fcols], wbuf.at[slot], local.at[2 + slot]
+                n.wud.at[:, flip(r, turn(tick // tiles)), :, fcols], wbuf.at[slot], local.at[slot]
             )
 
-        def c_copy(s, t):
+        def fetch_start(tick):
+            own = turn(tick // tiles) == 0
+
+            @pl.when(jnp.logical_not(own))
+            def _():
+                fetch(tick).start()
+
+            @pl.when(own)
+            def _():
+                fcols = pl.ds(pl.multiple_of(lax.rem(tick, tiles) * TF, TF), TF)
+                slot = lax.rem(tick, 2)
+                for kind in range(2):
+                    source = (n.w_up, n.w_down)[kind].at[:, fcols]
+                    pltpu.make_async_copy(source, wbuf.at[slot, kind, cols], local.at[slot]).start()
+                    for p in peers:
+                        rows = rows_of(col_at(p))
+                        pltpu.make_async_copy(
+                            n.wud.at[kind, r, rows, fcols], wbuf.at[slot, kind, rows], local.at[slot]
+                        ).start()
+
+        def c_copy(k, t):
             to = col_at(t)
             return remote(
-                gbuf.at[lax.rem(s, 2), :, rows_of(to)], n.crecv.at[s, t - 1], sem["c"], s * (C - 1) + t - 1, col=to
+                gbuf.at[lax.rem(k, 2), :, rows_of(to)], n.crecv.at[turn(k), t - 1], sem["c"], k * (C - 1) + t - 1,
+                col=to,
             )
 
         def o_copy(t):
             to = col_at(t)
-            return remote(obuf.at[:, rows_of(to)], n.orecv.at[t - 1], sem["o"], t - 1, col=to)
-
-        def join(s):
+            return remote(obuf.at[:, to], n.orecv.at[t - 1], sem["o"], t - 1, col=to)
+
+        def join(k):
+            s = turn(k)
             for t in peers:
-                c_copy(s, t).wait_recv()
+                c_copy(k, t).wait_recv()
             for kind in range(2):
-                total = gbuf[lax.rem(s, 2), kind, cols, :].astype(f32)
+                total = gbuf[lax.rem(k, 2), kind, cols, :].astype(f32)
                 for t in peers:
                     total = total + n.crecv[s, t - 1, kind].astype(f32)
                 n.crecv[s, 0, kind] = total.astype(bf16)
 
-        def send_row(s):
-            u_copy(s).start()
+            if z_first:
+                for g in groups:
+                    b_copy(s, g).start()
+
+            @pl.when(s > 0)
+            def _():
+                u_copy(s).start()
+                for kind in row_kinds:
+                    row_copy(s, kind).start()
+
+        for p in peers:
             for kind in range(2):
-                row_copy(s, kind).start()
-
-        own_up.wait()
-        own_down.wait()
-        for t in peers:
-            for kind in range(2):
-                gc_own(kind, t).wait()
-        fetch(0).start()
+                gc_copy(0, kind, p).wait()
+        fetch_start(0)
         cott[...] = n.cot[...].T
         for s in others:
             for t in peers:
@@ -401,9 +463,13 @@
         vsum = jnp.zeros((1, D), f32)
         for part in range(T // TR):
             rows = slice(part * TR, (part + 1) * TR)
-            branch = mm(n.att[0, rows, :], n.wo[0], NT)
-            for b in range(1, R):
-                branch += mm(n.att[b, rows, :], n.wo[b], NT)
+            branch = []
+            for device in range(C):
+                piece = mm(n.att[0, rows, :], n.wo[0, device], NN)
+                for b in range(1, R):
+                    piece += mm(n.att[b, rows, :], n.wo[b, device], NN)
+                branch.append(piece)
+            branch = jnp.concatenate(branch, axis=1)
             hidden = n.x[rows, :].astype(f32) + n.emb[0:1, :] + branch + vec(2)
             n.tgrad[rows, :] = hidden
             centred, inverse = normalize(hidden, D)
@@ -414,39 +480,39 @@
         n2t[...] = n2[...].T
         n.vbuf[5:6, :] = vsum
 
+        def second_half(s):
+            z_copy(s).wait_recv()
+            for p in peers:
+                gc_half(s, 1, p).start()
+
+        def arrived(s):
+            for p in peers:
+                for kind in range(2):
+                    gc_copy(s, kind, p).wait_recv()
+
         def tick_step(tick, carry):
-            s, t = tick // tiles, lax.rem(tick, tiles)
-            b = flip(r, s)
-            slot, wslot = lax.rem(s, 2), lax.rem(tick, 2)
+            k, t = tick // tiles, lax.rem(tick, tiles)
+            b = flip(r, turn(k))
+            slot, wslot = lax.rem(k, 2), lax.rem(tick, 2)
             fetch(tick).wait()
 
-            @pl.when((t == 0) & (s + 1 < R))
-            def _():
-                @pl.when(s == 0)
-                def _():
-                    g_copy(3).wait_recv()
-                    z_copy(3).start()
-                    for p in peers:
-                        gc_copy(3, 0, p).start()
-
-                z_copy(s + 1).wait_recv()
+            @pl.when((t == 0) & (k >= 2))
+            def _():
                 for p in peers:
-                    gc_copy(s + 1, 1, p).start()
-
-            @pl.when((t == 0) & (s >= 2))
-            def _():
-                for p in peers:
-                    c_copy(s - 2, p).wait_send()
-
-            @pl.when((t == tiles - 1) & (s + 1 < R))
-            def _():
-                for p in peers:
-                    gc_copy(s + 1, 0, p).wait_recv()
-                    gc_copy(s + 1, 1, p).wait_recv()
-
-            @pl.when(tick + 1 < ticks)
-            def _():
-                fetch(tick + 1).start()
+                    c_copy(k - 2, p).wait_send()
+
+            @pl.when(tick == 0)
+            def _():
+                half_on(2)
+
+            @pl.when(tick == tiles - 1)
+            def _():
+                second_half(3)
+                arrived(3)
+
+            @pl.when((t < tiles - 1) | (k == 0))
+            def _():
+                fetch_start(tick + 1)
 
             fcols = pl.ds(pl.multiple_of(t * TF, TF), TF)
             wu = wbuf[wslot, 0]
@@ -466,15 +532,19 @@
             @pl.when(t == tiles - 1)
             def _():
                 for p in peers:
-                    c_copy(s, p).start()
-
-            @pl.when((t == 0) & (s > 0))
-            def _():
-                join(s - 1)
-
-                @pl.when(s > 1)
-                def _():
-                    send_row(s - 1)
+                    c_copy(k, p).start()
+
+                for near, turn_before in ((1, 1), (2, 2)):
+
+                    @pl.when(k == turn_before)
+                    def _(near=near):
+                        second_half(near)
+                        arrived(near)
+                        fetch_start(tick + 1)
+
+            @pl.when((t == 0) & (k > 0))
+            def _():
+                join(k - 1)
 
             return carry
 
@@ -502,7 +572,11 @@
         def back_step(at, carry):
             s = R - 1 - at
             b = flip(r, s)
-            n.gsend[b] = mm(n2[...], n.wo[b], NN).astype(bf16)
+            grad = n2[...]
+            back = mm(lanes(grad, 0), n.wo[b, 0], NT)
+            for device in range(1, C):
+                back += mm(lanes(grad, device), n.wo[b, device], NT)
+            n.gsend[b] = back.astype(bf16)
 
             @pl.when(s > 0)
             def _():
@@ -512,12 +586,12 @@
 
         lax.fori_loop(0, R, back_step, 0)
         n.gatt[r] = n.gsend[r]
-        n2t[...] = n2[...].T
         join(R - 1)
-        send_row(R - 1)
 
         def out_step(b, carry):
-            obuf[b] = mm(n2t[...], n.att[b], NN).astype(bf16)
+            block = mm(n.att[b], n2[...], TN).astype(bf16)
+            for device in range(C):
+                obuf[b, device] = lanes(block, device)
             return carry
 
         lax.fori_loop(0, R, out_step, 0)
@@ -526,7 +600,7 @@
         for t in peers:
             o_copy(t).wait_recv()
         for b in range(R):
-            total = obuf[b, cols, :].astype(f32)
+            total = obuf[b, c].astype(f32)
             for t in peers:
                 total = total + n.orecv[t - 1, b].astype(f32)
             n.orecv[0, b] = total.astype(bf16)
@@ -541,35 +615,68 @@
     pl.run_scoped(
         middle,
         pltpu.VMEM((2, 2, D, TF), dt), pltpu.VMEM((T, D), f32), pltpu.VMEM((T, D), f32), pltpu.VMEM((T, D), dt),
-        pltpu.VMEM((D, T), dt), pltpu.VMEM((D, T), dt), pltpu.VMEM((2, 2, D, F), dt), pltpu.VMEM((R, D, H), dt),
+        pltpu.VMEM((D, T), dt), pltpu.VMEM((D, T), dt), pltpu.VMEM((2, 2, D, F), dt), pltpu.VMEM((R, C, H, DC), dt),
     )
 
-    DZ = n.zr.shape[2]
-    split = DZ != DC
     sources = (n.crecv.at[0, 0, 0], n.crecv.at[0, 0, 1], n.oblk, n.qblk)
-    landing = (n.zr.at[0], n.zr.at[1], n.zro, n.zrq)
+    landing = (n.zr.at[0], n.zr.at[n.zr.shape[0] - 1], n.zro, n.zrq)
     finals = (n.up_out, n.down_out, n.wo_out, n.qkv_out)
 
-    def part_of(device):
-        return pl.ds(pl.multiple_of(device * DZ, DZ), DZ) if split else slice(None)
+    heights = (DC, DC, H, 3 * H)
+    split = [landing[kind].shape[1] != heights[kind] for kind in range(4)]
+    def part_of(kind, device):
+        height = landing[kind].shape[1]
+        return pl.ds(pl.multiple_of(device * height, height), height) if split[kind] else slice(None)
 
     def zz_copy(kind, s):
         to = lax.rem(z + s, Z)
-        return remote(sources[kind].at[part_of(to)], landing[kind].at[s - 1], sem["z"], kind * (Z - 1) + s - 1, dp=to)
+        return remote(sources[kind].at[part_of(kind, to)], landing[kind].at[s - 1], sem["z"], kind * (Z - 1) + s - 1, dp=to)
 
     def y_copy(kind, s):
-        piece = finals[kind].at[part_of(z)]
+        piece = finals[kind].at[part_of(kind, z)]
         return remote(piece, piece, sem["y"], kind * (Z - 1) + s - 1, dp=lax.rem(z + s, Z))
 
+    def z_start(kind):
+        for s in groups:
+            zz_copy(kind, s).start()
+
+    def z_end(kind):
+        for s in groups:
+            zz_copy(kind, s).wait_recv()
+        total = sources[kind][part_of(kind, z), :].astype(f32)
+        for s in groups:
+            total = total + landing[kind][s - 1].astype(f32)
+        finals[kind][part_of(kind, z), :] = total.astype(bf16)
+        if split[kind]:
+            for s in groups:
+                y_copy(kind, s).start()
+
+    def down_end():
+        if not z_first:
+            z_end(1)
+            return
+        total = n.bsum[0].astype(f32)
+        for s in others:
+            br_copy(s).wait_recv()
+            total = total + n.brow[s - 1].astype(f32)
+        finals[1][b_part(z), :] = total.astype(bf16)
+        for s in groups:
+            y_copy(1, s).start()
+
+    def z_finish(kind):
+        for s in groups:
+            if kind != 1 or not z_first:
+                zz_copy(kind, s).wait_send()
+            if split[kind]:
+                y_copy(kind, s).wait()
+
     def row_sum(kind):
+        total = n.crecv[0, 0, kind].astype(f32)
         for s in others:
             row_copy(s, kind).wait_recv()
-        total = n.crecv[0, 0, kind].astype(f32)
-        for s in others:
             total = total + n.grow[s - 1, kind].astype(f32)
         n.crecv[0, 0, kind] = total.astype(bf16)
-        for s in groups:
-            zz_copy(kind, s).start()
+        z_start(kind)
 
     def wrow_sum():
         for s in others:
@@ -578,19 +685,7 @@
         for s in others:
             total = total + n.orow[s - 1].astype(f32)
         n.oblk[...] = total.astype(bf16)
-        for s in groups:
-            zz_copy(2, s).start()
-
-    def data_sum(kind):
-        for s in groups:
-            zz_copy(kind, s).wait_recv()
-        total = sources[kind][part_of(z), :].astype(f32)
-        for s in groups:
-            total = total + landing[kind][s - 1].astype(f32)
-        finals[kind][part_of(z), :] = total.astype(bf16)
-        if split:
-            for s in groups:
-                y_copy(kind, s).start()
+        z_start(2)
 
     def p_copy(link, part, b):
         piece = pl.ds(part * half, half)
@@ -639,7 +734,9 @@
                 axis=1,
             ).astype(bf16)
             gp[b] = stack
-            n.part[b] = mm(stack, n.wq[...], NT).astype(bf16)
+            n.part[b] = jnp.concatenate(
+                [mm(stack, n.wq[device], NN).astype(bf16) for device in range(C)], axis=1
+            )
             s = flip(r, b)
 
             @pl.when(s == 3)
@@ -686,8 +783,13 @@
             finish(i)
             if i + 1 < R:
                 combine(i + 1)
+            else:
+                b_sum(0)
+                b_sum(3)
+                b_sum(1)
         for i in range(early - 1, -1, -1):
             spread(i)
+        b_sum(2)
         row_sum(0)
 
         def square(t, carry):
@@ -695,47 +797,50 @@
             pair(t // (early * early), rest // early, lax.rem(rest, early), True)
             return carry
 
-        lax.fori_loop(0, heads * early * early, square, 0)
+        total = heads * early * early
+        lax.fori_loop(0, total // 2, square, 0)
+        if not z_first:
+            row_sum(1)
+        wrow_sum()
+        lax.fori_loop(total // 2, total, square, 0)
+        down_end()
         for b in range(early - 1, -1, -1):
             finish(b)
         combine(early)
-        row_sum(1)
-        wrow_sum()
 
         qg[...] = jnp.zeros_like(qg)
 
         def qkv_step(b, carry):
-            qg[...] += mm(n.one[b], gp[b], TN)
+            qg[...] += mm(gp[b], n.one[b], TN)
             return carry
 
         lax.fori_loop(0, R, qkv_step, 0)
-        n.qgb[...] = qg[...].astype(bf16)
+        for device in range(C):
+            n.wq[device] = lanes(qg, device).astype(bf16)
 
         def q_copy(t):
             to = col_at(t)
-            return remote(n.qgb.at[rows_of(to)], n.qrecv.at[t - 1], sem["q"], t - 1, col=to)
+            return remote(n.wq.at[to], n.qrecv.at[t - 1], sem["q"], t - 1, col=to)
 
         for t in peers:
             q_copy(t).start()
         for b in range(early - 1, -1, -1):
             combine(b)
-        data_sum(0)
+        z_end(0)
+        z_end(2)
         for t in peers:
             q_copy(t).wait()
-        total = n.qgb[cols, :].astype(f32)
+        total = n.wq[c].astype(f32)
         for t in peers:
             total = total + n.qrecv[t - 1].astype(f32)
         n.qblk[...] = total.astype(bf16)
-        for s in groups:
-            zz_copy(3, s).start()
+        z_start(3)
 
     pl.run_scoped(
         back,
         pltpu.VMEM((heads, L, LANES), bf16), pltpu.VMEM((heads, L, LANES), f32), pltpu.VMEM((heads, L, LANES), f32),
-        pltpu.VMEM((heads, L, LANES), f32), pltpu.VMEM((R, T, 3 * H), bf16), pltpu.VMEM((D, 3 * H), f32),
+        pltpu.VMEM((heads, L, LANES), f32), pltpu.VMEM((R, T, 3 * H), bf16), pltpu.VMEM((3 * H, D), f32),
     )
-    data_sum(1)
-    data_sum(2)
 
     for link in range(2):
         for part in range(2):
@@ -761,12 +866,11 @@
     def v_copy(s):
         return remote(n.vbuf, n.vrow.at[s - 1], sem["v"], s - 1, row=flip(r, s))
 
-    def vc_copy(t):
-        return remote(n.vcol.at[c], n.vcol.at[c], sem["vc"], t - 1, col=col_at(t))
-
-    def vz_copy(s):
-        return remote(n.vcol, n.vz.at[s - 1], sem["vz"], s - 1, dp=lax.rem(z + s, Z))
-
+    def all_copy(s, t):
+        piece = n.vall.at[z, c]
+        return remote(piece, piece, sem["vz"], s * C + t - 1, dp=lax.rem(z + s, Z), col=col_at(t))
+
+    rest = [(s, t) for s in range(Z) for t in range(C) if s + t > 0]
     for s in others:
         v_copy(s).start()
     up_bias = n.ubg[r]
@@ -778,26 +882,21 @@
     total = n.vbuf[...]
     for s in others:
         total = total + n.vrow[s - 1]
-    n.vcol[c, 0:8, :] = total
-    n.vcol[c, 7:8, :] = up_bias
-    n.vcol[c, 8:16, :] = jnp.full((8, D), n.stamp[0].astype(f32))
-    for t in peers:
-        vc_copy(t).start()
-    for t in peers:
-        vc_copy(t).wait_recv()
-    for s in groups:
-        vz_copy(s).start()
-    data_sum(3)
-    for s in groups:
-        vz_copy(s).wait_recv()
+    n.vall[z, c, 0:8, :] = total
+    n.vall[z, c, 7:8, :] = up_bias
+    n.vall[z, c, 8:16, :] = jnp.full((8, D), n.stamp[0].astype(f32))
+    for s, t in rest:
+        all_copy(s, t).start()
+    z_end(3)
+    for s, t in rest:
+        all_copy(s, t).wait_recv()
     total = jnp.zeros((8, D), f32)
     number = (lax.broadcasted_iota(jnp.int32, (NTB, D), 0) + c * NTB).astype(f32)
     table = jnp.zeros((NTB, D), f32)
     for s in range(Z):
         for t in range(C):
-            entry = n.vcol[t] if s == 0 else n.vz[s - 1, t]
-            total = total + entry[0:8]
-            table = table + jnp.where(number == entry[8:9], entry[6:7], 0.0)
+            total = total + n.vall[s, t, 0:8, :]
+            table = table + jnp.where(number == n.vall[s, t, 8:9, :], n.vall[s, t, 6:7, :], 0.0)
     n.small[...] = total
     n.table_out[...] = table
 
@@ -805,7 +904,6 @@
         stamp_copy(t).wait_send()
         pick_copy(t).wait_send()
         w_copy(t).wait_send()
-        vc_copy(t).wait_send()
         for s in range(R):
             woc_copy(s, t).wait_send()
             if s > 0:
@@ -818,50 +916,57 @@
             n_copy(link, part).wait_send()
             p_copy(link, part, 0).wait_send()
     for s in others:
-        for copy in (a_copy, g_copy, z_copy, wo_copy, ub_copy, a2_copy, wrow_copy, u_copy, v_copy):
+        half_copy(s, 0).wait_send()
+        for copy in (a_copy, z_copy, wo_copy, ub_copy, a2_copy, wrow_copy, u_copy, v_copy):
             copy(s).wait_send()
-        for kind in range(2):
+        for kind in row_kinds:
             row_copy(s, kind).wait_send()
-    for s in groups:
-        vz_copy(s).wait_send()
-        for kind in range(4):
-            zz_copy(kind, s).wait_send()
-            if split:
-                y_copy(kind, s).wait()
+        if z_first:
+            br_copy(s).wait_send()
+    if z_first:
+        for s in range(R):
+            for g in groups:
+                b_copy(s, g).wait_send()
+    for s, t in rest:
+        all_copy(s, t).wait_send()
+    for kind in range(4):
+        z_finish(kind)
 
 
 def run_layer(C, Z, stamp, prefix, x, cot, table, vectors, w_qkv, w_out, w_up, w_down):
     T, D = x.shape
     DC, F = w_up.shape
-    H = w_out.shape[1]
+    H = w_out.shape[0]
     heads = H // HD
     L = R * T
     NTB = table.shape[0]
-    DZ = DC // Z if DC % (16 * Z) == 0 else DC
+    part = lambda height: height // Z if height % (16 * Z) == 0 else height
+    kinds, rows_b = (1, DC // Z) if DC % (16 * Z) == 0 else (2, 16)
     vm = pltpu.VMEM
-    ins = dict(stamp=SM, prefix=SM, x=VM, cot=VM, table=VM, vectors=VM, w_qkv=VM, w_out=VM, w_up=AN, w_down=AN)
+    given = ("ln1_gain", "ln1_bias", "out_bias", "ln2_gain", "ln2_bias", "down_bias", "up_bias")
+    ins = dict(stamp=SM, prefix=SM, x=VM, cot=VM, table=VM, **{name: VM for name in given}, w_qkv=VM, w_out=VM, w_up=AN, w_down=AN)
     outs = dict(
         out=((T, D), bf16), tgrad=((T, D), f32), up_out=((DC, F), bf16), down_out=((DC, F), bf16),
-        wo_out=((DC, H), bf16), qkv_out=((DC, 3 * H), bf16), small=((8, D), f32), table_out=((NTB, D), f32),
+        wo_out=((H, DC), bf16), qkv_out=((3 * H, DC), bf16), small=((8, D), f32), table_out=((NTB, D), f32),
         wud=((2, R, D, F), bf16),
     )
     scratch = dict(
         stamp_own=vm((8, LANES), f32), stamp_got=vm((C - 1, 8, LANES), f32), picked=vm((C - 1, 8, D), f32),
-        picked_got=vm((C - 1, 8, D), f32), emb=vm((8, D), f32), wq=vm((D, 3 * H), bf16), one=vm((R, T, D), bf16),
+        picked_got=vm((C - 1, 8, D), f32), emb=vm((8, D), f32), vectors=vm((8, D), f32), wq=vm((C, 3 * H, DC), bf16), one=vm((R, T, D), bf16),
         q=vm((heads, L, LANES), bf16), k=vm((heads, L, LANES), bf16), v=vm((heads, L, LANES), bf16),
-        mine=vm((R, T, H), bf16), att=vm((R, T, H), bf16), wo=vm((R, D, H), bf16),
+        mine=vm((R, T, H), bf16), att=vm((R, T, H), bf16), wo=vm((R, C, H, DC), bf16),
         ub=vm((R, 8, F), f32), vbuf=vm((8, D), f32), ubg=vm((R, 1, F), f32),
-        crecv=vm((R, C - 1, 2, DC, F), bf16), orecv=vm((C - 1, R, DC, H), bf16), gsend=vm((R, T, H), bf16),
-        gatt=vm((R, T, H), bf16), grow=vm((R - 1, 2, DC, F), bf16), orow=vm((R - 1, DC, H), bf16),
-        urow=vm((R - 1, 1, F), f32), part=vm((R, T, D), bf16), prec=vm((2, T, D), bf16), prel=vm((2, T // 2, D), bf16),
-        qgb=vm((D, 3 * H), bf16), qrecv=vm((C - 1, DC, 3 * H), bf16), oblk=vm((DC, H), bf16), qblk=vm((DC, 3 * H), bf16),
-        zr=vm((2, Z - 1, DZ, F), bf16), zro=vm((Z - 1, DZ, H), bf16), zrq=vm((Z - 1, DZ, 3 * H), bf16),
-        vrow=vm((R - 1, 8, D), f32), vcol=vm((C, 16, D), f32), vz=vm((Z - 1, C, 16, D), f32),
+        crecv=vm((R, C - 1, 2, DC, F), bf16), orecv=vm((C - 1, R, H, DC), bf16), gsend=vm((R, T, H), bf16),
+        gatt=vm((R, T, H), bf16), grow=vm((R - 1, kinds, DC, F), bf16), orow=vm((R - 1, H, DC), bf16),
+        urow=vm((R - 1, 1, F), f32), bz=vm((R, Z - 1, rows_b, F), bf16), bsum=vm((R, rows_b, F), bf16), brow=vm((R - 1, rows_b, F), bf16), part=vm((R, T, D), bf16), prec=vm((2, T, D), bf16), prel=vm((2, T // 2, D), bf16),
+        qrecv=vm((C - 1, 3 * H, DC), bf16), oblk=vm((H, DC), bf16), qblk=vm((3 * H, DC), bf16),
+        zr=vm((kinds, Z - 1, part(DC), F), bf16), zro=vm((Z - 1, part(H), DC), bf16), zrq=vm((Z - 1, part(3 * H), DC), bf16),
+        vrow=vm((R - 1, 8, D), f32), vall=vm((Z, C, 16, D), f32),
     )
     sems = dict(
-        stamp=C - 1, pick=C - 1, w=C - 1, n=4, relay=2, g=R - 1, gz=R - 1, gc=2 * R * (C - 1), wo=R - 1,
+        stamp=C - 1, pick=C - 1, w=C - 1, n=4, relay=2, g=R - 1, gz=R - 1, b=R * (Z - 1), br=R - 1, gc=2 * R * (C - 1), wo=R - 1,
         woc=R * (C - 1), ub=R - 1, a=R - 1, a2=R - 1, row=2 * (R - 1), wrow=R - 1, u=R - 1, c=R * (C - 1), o=C - 1,
-        z=4 * (Z - 1), y=4 * (Z - 1), p=4, pr=2, q=C - 1, v=R - 1, vc=C - 1, vz=Z - 1,
+        z=4 * (Z - 1), y=4 * (Z - 1), p=4, pr=2, q=C - 1, v=R - 1, vz=Z * C - 1,
     )
     names = list(ins) + list(outs) + list(scratch) + ["sem_" + name for name in sems]
     dma = pltpu.SemaphoreType.DMA
@@ -873,10 +978,10 @@
         out_shape=tuple(jax.ShapeDtypeStruct(*spec) for spec in outs.values()),
         in_specs=list(ins.values()),
         out_specs=(VM,) * (len(outs) - 1) + (AN,),
-        scratch_shapes=list(scratch.values()) + semaphores + [dma((4,))],
+        scratch_shapes=list(scratch.values()) + semaphores + [dma((2,))],
         compiler_params=pltpu.CompilerParams(collective_id=0, has_side_effects=True, vmem_limit_bytes=67043328),
         name="layer",
-    )(stamp, prefix, x, cot, table, vectors, w_qkv, w_out, w_up, w_down)
+    )(stamp, prefix, x, cot, table, *vectors, w_qkv, w_out, w_up, w_down)
     return dict(zip(outs, results))
 
 
@@ -884,15 +989,15 @@
     (tokens, cotangent, timesteps, prefix_len, time_table, ln1_gain, ln1_bias, w_qkv, w_out, out_bias,
      ln2_gain, ln2_bias, w_up, up_bias, w_down, down_bias) = args
     DC, _, H = w_qkv.shape
-    vectors = jnp.stack([ln1_gain, ln1_bias, out_bias, ln2_gain, ln2_bias, down_bias, up_bias, up_bias])
+    vectors = (ln1_gain, ln1_bias, out_bias, ln2_gain, ln2_bias, down_bias, up_bias)
     o = run_layer(
-        C, Z, timesteps, prefix_len, tokens[0], cotangent[0], time_table, vectors, w_qkv.reshape(DC, 3 * H), w_out,
-        w_up, w_down,
+        C, Z, timesteps, prefix_len, tokens[0], cotangent[0], time_table, vectors,
+        w_qkv.transpose(1, 2, 0).reshape(3 * H, DC), w_out.T, w_up, w_down,
     )
     small = o["small"]
     return (
         o["out"][None], o["tgrad"][None], o["table_out"], small[0], small[1],
-        o["qkv_out"].astype(f32).reshape(DC, 3, H), o["wo_out"].astype(f32), small[2], small[3], small[4],
+        o["qkv_out"].astype(f32).reshape(3, H, DC).transpose(2, 0, 1), o["wo_out"].astype(f32).T, small[2], small[3], small[4],
         o["up_out"].astype(f32), small[7], o["down_out"].astype(f32), small[5],
     )
 

time: 315 us -> 264 us (0.84)
  the two profiles are of different devices: /device:TPU:26 before, /device:TPU:11 now
where the time goes in v4:
time: 264 us
  Pallas kernels  250 us (95%)
  other arithmetic  5.87 us (2%)
  local copies, waits for them, and re-layouts  5.82 us (2%)
    pallas_call x1, Pallas kernels, run_layer(): pl.pallas_call(functools.partial(layer_kernel, names, C, Z), out_shape=tu...  250 us

profile of v4, /device:TPU:11, one launch (start us, length us, event | category | flops | bytes accessed | tf_op | source)
XLA Modules:
  0.0 263.5 jit_solution(1992338368288732122)
XLA Ops:
  1.9 249.9 %layer.1 = (bf16[512,768]{1,0:T(8,128)(2,1)}, f32[512,768]{1,0:T(8,128)}, bf16[384,768]{1,0:T(8,128)(2,1)}, bf16[384,768]{1,0:T(8,128)(2,1)}, bf16[192,384]{1,0:...) custom-call(s32[1]{0:T(128)S(6)} %copy.33.refs_0_, ...), custom_call_target="tpu_custom_call" | custom-call | tf_op jit(solution)/shard_map/layer/pallas_call | solution.py:976
  251.8 0.0 copy-start.4
  251.8 1.8 slice_reduce_fusion
  253.6 1.6 convert_bitcast_fusion.1
  255.3 0.0 copy-start.3
  255.3 2.0 convert_bitcast_fusion
  257.3 0.0 copy-done.4
  257.3 0.0 copy-start.2
  257.3 1.1 convert_element_type.8
  258.4 0.0 copy-done.3
  258.4 0.0 copy-start
  258.4 1.1 convert_element_type.9
  259.5 0.0 copy-done.2
  259.5 0.9 copy.35
  260.4 0.0 copy-done
  260.4 0.0 copy-start.1
  260.4 1.1 copy.36
  261.6 0.8 copy-done.1
  262.4 1.1 copy.37
Async XLA Ops:
  251.8 5.5 %copy-start.4 = (bf16[384,768]{1,0:T(8,128)(2,1)S(1)}, bf16[384,768]{1,0:T(8,128)(2,1)}, u32[]{:S(2)}) copy-start(bf16[384,768]{1,0:T(8,128)(2,1)} %get-tuple-element.28) | copy-start | bytes 1769476
  255.3 3.1 %copy-start.3 = (bf16[384,768]{1,0:T(8,128)(2,1)S(1)}, bf16[384,768]{1,0:T(8,128)(2,1)}, u32[]{:S(2)}) copy-start(bf16[384,768]{1,0:T(8,128)(2,1)} %get-tuple-element.29) | copy-start | bytes 1769476
  257.3 2.2 copy-start.2
  258.4 2.0 copy-start
  260.4 2.0 copy-start.1

commit v5 on v4

--- a/solution.py
+++ b/solution.py
@@ -326,8 +326,7 @@
                         for t in peers:
                             woc_copy(s, t).start()
                     half_start(1)
-                    half_start(2)
-                if at == 2:
+                if at == 1:
                     half_on(3)
 
         return carry
@@ -337,6 +336,7 @@
         lax.fori_loop(0, R, attend_block, 0)
 
     pl.run_scoped(attend_all, pltpu.VMEM((heads, T, LANES), f32))
+    half_start(2)
     n.att[r] = n.mine[r]
     half_on(1)
 
@@ -501,12 +501,9 @@
                 for p in peers:
                     c_copy(k - 2, p).wait_send()
 
-            @pl.when(tick == 0)
+            @pl.when(tick == tiles - 1)
             def _():
                 half_on(2)
-
-            @pl.when(tick == tiles - 1)
-            def _():
                 second_half(3)
                 arrived(3)
 
@@ -797,16 +794,36 @@
             pair(t // (early * early), rest // early, lax.rem(rest, early), True)
             return carry
 
-        total = heads * early * early
-        lax.fori_loop(0, total // 2, square, 0)
+        def corner(t, carry):
+            rest = lax.rem(t, 3)
+            pair(t // 3, 1 - rest // 2, (rest + 1) // 2 - rest // 2 + rest // 2, True)
+            return carry
+
+        def origin(h, carry):
+            pair(h, 0, 0, True)
+            return carry
+
+        if early == 2:
+            lax.fori_loop(0, 3 * heads // 2, corner, 0)
+        else:
+            lax.fori_loop(0, heads * early * early, square, 0)
         if not z_first:
             row_sum(1)
         wrow_sum()
-        lax.fori_loop(total // 2, total, square, 0)
-        down_end()
-        for b in range(early - 1, -1, -1):
-            finish(b)
-        combine(early)
+        if early == 2:
+            lax.fori_loop(3 * heads // 2, 3 * heads, corner, 0)
+            down_end()
+            finish(1)
+            combine(2)
+            lax.fori_loop(0, heads, origin, 0)
+            finish(0)
+            z_end(0)
+        else:
+            for b in range(early - 1, -1, -1):
+                finish(b)
+            combine(early)
+            down_end()
+            z_end(0)
 
         qg[...] = jnp.zeros_like(qg)
 
@@ -826,7 +843,6 @@
             q_copy(t).start()
         for b in range(early - 1, -1, -1):
             combine(b)
-        z_end(0)
         z_end(2)
         for t in peers:
             q_copy(t).wait()
@@ -985,6 +1001,47 @@
     return dict(zip(outs, results))
 
 
+def tail_kernel(out, tgrad, table, small, up, down, wo, qkv, *refs):
+    refs[0][...] = out[...]
+    refs[1][...] = tgrad[...]
+    for source, target in zip((up, down, wo, qkv), refs[3:7]):
+        target[...] = source[...].astype(f32)
+
+    @pl.when(pl.program_id(0) == 0)
+    def _():
+        refs[2][...] = table[...]
+        for row in range(8):
+            if row != 6:
+                target = refs[7 + (row if row < 6 else 6)]
+                target[...] = small[row : row + 1, :].reshape(target.shape[0])
+
+
+def run_tail(o):
+    steps = 4
+    arrays = [o[name] for name in ("out", "tgrad", "table_out", "small", "up_out", "down_out", "wo_out", "qkv_out")]
+
+    def rows(array):
+        return pl.BlockSpec((array.shape[0] // steps, array.shape[1]), lambda i: (i, 0))
+
+    def whole(array):
+        return pl.BlockSpec(array.shape, lambda i: (0, 0))
+
+    ins = [whole(array) if i in (2, 3) else rows(array) for i, array in enumerate(arrays)]
+    width = arrays[3].shape[1]
+    line = pl.BlockSpec((width,), lambda i: (0,))
+    chosen = (0, 1, 2, 4, 5, 6, 7)
+    kinds = [arrays[i].dtype if i < 4 else f32 for i in chosen]
+    return pl.pallas_call(
+        tail_kernel,
+        grid=(steps,),
+        out_shape=[jax.ShapeDtypeStruct(arrays[i].shape, kind) for i, kind in zip(chosen, kinds)]
+        + [jax.ShapeDtypeStruct((width,), f32)] * 7,
+        in_specs=ins,
+        out_specs=[ins[i] for i in chosen] + [line] * 7,
+        name="results",
+    )(*arrays)
+
+
 def body(C, Z, *args):
     (tokens, cotangent, timesteps, prefix_len, time_table, ln1_gain, ln1_bias, w_qkv, w_out, out_bias,
      ln2_gain, ln2_bias, w_up, up_bias, w_down, down_bias) = args
@@ -994,11 +1051,10 @@
         C, Z, timesteps, prefix_len, tokens[0], cotangent[0], time_table, vectors,
         w_qkv.transpose(1, 2, 0).reshape(3 * H, DC), w_out.T, w_up, w_down,
     )
-    small = o["small"]
+    out, tgrad, table, up, down, wo, qkv, gain1, bias1, bias_out, gain2, bias2, bias_down, bias_up = run_tail(o)
     return (
-        o["out"][None], o["tgrad"][None], o["table_out"], small[0], small[1],
-        o["qkv_out"].astype(f32).reshape(3, H, DC).transpose(2, 0, 1), o["wo_out"].astype(f32).T, small[2], small[3], small[4],
-        o["up_out"].astype(f32), small[7], o["down_out"].astype(f32), small[5],
+        out[None], tgrad[None], table, gain1, bias1, qkv.reshape(3, H, DC).transpose(2, 0, 1), wo.T, bias_out, gain2,
+        bias2, up, bias_up, down, bias_down,
     )
 
 

time: 264 us -> 255 us (0.966)
  the two profiles are of different devices: /device:TPU:11 before, /device:TPU:15 now
where the time goes in v5:
time: 255 us; the launch traced here: 254 us
  Pallas kernels  252 us (99%)
    pallas_call x1, Pallas kernels, run_layer(): pl.pallas_call(functools.partial(layer_kernel, names, C, Z), out_shape=tu...  246 us
    pallas_call x1, Pallas kernels, run_tail(): pl.pallas_call(tail_kernel, grid=(steps,), out_shape=[jax.ShapeDtypeStruc...  6.6 us

profile of v5, /device:TPU:15, one launch (start us, length us, event | category | flops | bytes accessed | tf_op | source)
XLA Modules:
  0.0 254.4 jit_solution(7137163439447854348)
XLA Ops:
  1.9 245.7 %layer.1 = (bf16[512,768]{1,0:T(8,128)(2,1)}, f32[512,768]{1,0:T(8,128)}, bf16[384,768]{1,0:T(8,128)(2,1)}, bf16[384,768]{1,0:T(8,128)(2,1)}, bf16[192,384]{1,0:...) custom-call(s32[1]{0:T(128)S(6)} %copy.30.refs_0_, ...), custom_call_target="tpu_custom_call" | custom-call | tf_op jit(solution)/shard_map/layer/pallas_call | solution.py:992
  247.6 6.6 %results.1 = (bf16[512,768]{1,0:T(8,128)(2,1)}, f32[512,768]{1,0:T(8,128)}, f32[500,768]{1,0:T(8,128)}, f32[384,768]{1,0:T(8,128)}, f32[384,768]{1,0:T(8,128)}, ...) custom-call(bf16[512,768]{1,0:T(8,128)(2,1)} %get-tuple-element.36.o, ...), custom_call_target="tpu_custom_call" | custom-call | tf_op jit(solution)/shard_map/results/pallas_call | solution.py:1034

commit v6 on v5

--- a/solution.py
+++ b/solution.py
@@ -39,7 +39,7 @@
     return a0 + b0 - 2 * a0 * b0 + 2 * (a1 + b1 - 2 * a1 * b1)
 
 
-def greet(sizes):
+def greet(sizes, local_work):
     barrier = pltpu.get_barrier_semaphore()
     total = 0
     for name, count in sizes.items():
@@ -52,6 +52,7 @@
             to = {"dp": lax.rem(lax.axis_index("dp") + s, sizes["dp"]), "col": lax.rem(lax.axis_index("col") + t, sizes["col"])}
             pl.semaphore_signal(barrier, inc=1, device_id=to, device_id_type=MESH)
             total += 1
+    local_work()
     pl.semaphore_wait(barrier, total)
 
 
@@ -102,8 +103,6 @@
     cols = pl.ds(pl.multiple_of(c * DC, DC), DC)
     vec = lambda row: n.vectors[row : row + 1, :]
     given = (n.ln1_gain, n.ln1_bias, n.out_bias, n.ln2_gain, n.ln2_bias, n.down_bias, n.up_bias)
-    for row, ref in enumerate(given):
-        n.vectors[row : row + 1, :] = ref[...].reshape(1, D)
     others = range(1, R)
     peers = range(1, C)
     groups = range(1, Z)
@@ -117,7 +116,20 @@
     def rows_of(device):
         return pl.ds(pl.multiple_of(device * DC, DC), DC)
 
-    greet({"row": R, "col": C, "dp": Z})
+    def row_of(stamps):
+        number = (lax.broadcasted_iota(jnp.int32, (NTB, D), 0) + c * NTB).astype(f32)
+        return jnp.sum(jnp.where(number == stamps, n.table[...].astype(f32), 0.0), axis=0, keepdims=True)
+
+    def prepare():
+        for row, ref in enumerate(given):
+            n.vectors[row : row + 1, :] = ref[...].reshape(1, D)
+        n.stamp_own[...] = jnp.full(n.stamp_own.shape, n.stamp[0].astype(f32))
+        n.ub[r] = jnp.broadcast_to(vec(6), (8, F))
+        n.wo[r, c] = n.w_out[...]
+        n.wq[c] = n.w_qkv[...]
+        n.emb[...] = jnp.broadcast_to(row_of(n.stamp_own[0:1, 0:1]), n.emb.shape)
+
+    greet({"row": R, "col": C, "dp": Z}, prepare)
 
     def wo_copy(s):
         piece = n.wo.at[r, c]
@@ -131,8 +143,6 @@
     def ub_copy(s):
         return remote(n.ub.at[r], n.ub.at[r], sem["ub"], s - 1, row=flip(r, s))
 
-    n.ub[r] = jnp.broadcast_to(vec(6), (8, F))
-    n.wo[r, c] = n.w_out[...]
     for s in others:
         wo_copy(s).start()
         ub_copy(s).start()
@@ -148,22 +158,16 @@
     def w_copy(t):
         return remote(n.w_qkv, n.wq.at[c], sem["w"], t - 1, col=col_at(t))
 
-    n.stamp_own[...] = jnp.full(n.stamp_own.shape, n.stamp[0].astype(f32))
     for t in peers:
         stamp_copy(t).start()
     for t in peers:
         w_copy(t).start()
-    n.wq[c] = n.w_qkv[...]
-
-    def row_of(stamps):
-        number = (lax.broadcasted_iota(jnp.int32, (NTB, D), 0) + c * NTB).astype(f32)
-        return jnp.sum(jnp.where(number == stamps, n.table[...].astype(f32), 0.0), axis=0, keepdims=True)
 
     for t in peers:
         stamp_copy(t).wait_recv()
         n.picked[t - 1] = jnp.broadcast_to(row_of(n.stamp_got[t - 1][0:1, 0:1]), (8, D))
         pick_copy(t).start()
-    embed = row_of(n.stamp_own[0:1, 0:1])
+    embed = n.emb[0:1, :]
     for t in peers:
         pick_copy(t).wait_recv()
         embed = embed + n.picked_got[t - 1][0:1]

time: 255 us -> 255 us (level)
  no operation moved by 1% of the time
where the time goes in v6:
time: 255 us
  Pallas kernels  252 us (99%)
    pallas_call x1, Pallas kernels, run_layer(): pl.pallas_call(functools.partial(layer_kernel, names, C, Z), out_shape=tu...  246 us
    pallas_call x1, Pallas kernels, run_tail(): pl.pallas_call(tail_kernel, grid=(steps,), out_shape=[jax.ShapeDtypeStruc...  6.6 us

profile of v6, /device:TPU:15, one launch (start us, length us, event | category | flops | bytes accessed | tf_op | source)
XLA Modules:
  0.0 254.5 jit_solution(17194781991797103045)
XLA Ops:
  1.9 245.8 %layer.1 = (bf16[512,768]{1,0:T(8,128)(2,1)}, f32[512,768]{1,0:T(8,128)}, bf16[384,768]{1,0:T(8,128)(2,1)}, bf16[384,768]{1,0:T(8,128)(2,1)}, bf16[192,384]{1,0:...) custom-call(s32[1]{0:T(128)S(6)} %copy.30.refs_0_, ...), custom_call_target="tpu_custom_call" | custom-call | tf_op jit(solution)/shard_map/layer/pallas_call | solution.py:996
  247.7 6.6 %results.1 = (bf16[512,768]{1,0:T(8,128)(2,1)}, f32[512,768]{1,0:T(8,128)}, f32[500,768]{1,0:T(8,128)}, f32[384,768]{1,0:T(8,128)}, f32[384,768]{1,0:T(8,128)}, ...) custom-call(bf16[512,768]{1,0:T(8,128)(2,1)} %get-tuple-element.36.o, ...), custom_call_target="tpu_custom_call" | custom-call | tf_op jit(solution)/shard_map/results/pallas_call | solution.py:1038
